TPU v7x, 32 devices: a whole 2x2x4 slice. The times are simulated.
32 devices in a mesh: dp: 8 (over z, x), mp: 4 (over y, core).
Axes of the slice: x: 2, y: 2, z: 4, core: 2. Of those that a mesh axis runs over, the one named last changes fastest.
Arguments:
- tokens: bfloat16 [4096, 768], P(('dp', 'mp')), may hold values from -6 to 6
- cotangent: bfloat16 [4096, 768], P(('dp', 'mp')), may hold values from -6 to 6
- attn_gain: bfloat16 [768], P('dp'), may hold values from 0.25 to 1.75
- w_qkv: bfloat16 [768, 3, 768], P('dp', None, 'mp'), as said below
- w_attn_out: bfloat16 [768, 768], P('mp', 'dp'), may hold values from -2.5 to 2.5
- mlp_gain: bfloat16 [768], P('dp'), may hold values from 0.25 to 1.75
- w_in: bfloat16 [768, 2, 1152], P('dp', None, 'mp'), may hold values from -0.21875 to 0.21875
- w_mlp_out: bfloat16 [1152, 768], P('mp', 'dp'), may hold values from -0.1875 to 0.1875
Outputs:
- output: float32 [4096, 768], P(('dp', 'mp'))
- tokens_grad: float32 [4096, 768], P(('dp', 'mp'))
- attn_gain_grad: float32 [768], P('dp')
- w_qkv_grad: float32 [768, 3, 768], P('dp', None, 'mp')
- w_attn_out_grad: float32 [768, 768], P('mp', 'dp')
- mlp_gain_grad: float32 [768], P('dp')
- w_in_grad: float32 [768, 2, 1152], P('dp', None, 'mp')
- w_mlp_out_grad: float32 [1152, 768], P('mp', 'dp')
Inputs may be any that keep to these rules, and one draw needn't show every extreme that they name: Entries of w_qkv lie within plus or minus 8 / sqrt(768).
All inputs are finite; a program needn't handle non-finite values.
Results may differ from a plain program's by a relative error of at most 0.015.
Values may be sent and summed in bfloat16 or wider, within the bound.
A program may use at most 64 MiB of HBM per device.

v0:
```python
import jax
import jax.numpy as jnp
from jax import lax
from jax.sharding import PartitionSpec as P

HEAD_DIM = 64


norm_eps = 1e-05
rope_base = 160000.0
query_block = 512


def rotary_tables(length, head_width):
    half_width = head_width // 2
    freqs = rope_base ** (-(jnp.arange(half_width, dtype=jnp.float32) * 2.0 / head_width))
    angles = jnp.arange(length, dtype=jnp.float32)[:, None] * freqs[None, :]
    angles = jnp.concatenate([angles, angles], axis=1)
    return (jnp.cos(angles), jnp.sin(angles))


def rotate_half(values):
    half_width = values.shape[-1] // 2
    return jnp.concatenate([-values[..., half_width:], values[..., :half_width]], axis=-1)


def apply_rotary(values, cosine_table, sine_table):
    return values * cosine_table[:, None, :] + rotate_half(values) * sine_table[:, None, :]


def undo_rotary(grads, cosine_table, sine_table):
    return grads * cosine_table[:, None, :] - rotate_half(grads * sine_table[:, None, :])


def norm_stats(values):
    centered = values - jnp.mean(values, axis=-1, keepdims=True)
    variance = jnp.mean(centered * centered, axis=-1, keepdims=True)
    inverse = lax.rsqrt(variance + norm_eps)
    return (centered * inverse, inverse)


def norm_backward(grad_out, normed, inverse, gain_vals):
    scaled = grad_out * gain_vals
    grad_in = inverse * (
        scaled
        - jnp.mean(scaled, axis=-1, keepdims=True)
        - normed * jnp.mean(scaled * normed, axis=-1, keepdims=True)
    )
    return (grad_in, jnp.sum(grad_out * normed, axis=0))


def gelu_exact(values):
    return 0.5 * values * (1.0 + jax.scipy.special.erf(values * 0.7071067811865476))


def gelu_slope(values):
    return (
        0.5 * (1.0 + jax.scipy.special.erf(values * 0.7071067811865476))
        + values * jnp.exp(-0.5 * values * values) * 0.3989422804014327
    )


def contract_rows(left, right):
    return lax.dot_general(
        left, right, (((0,), (0,)), ((), ())), preferred_element_type=jnp.float32
    )


def times_transposed(left, right):
    return lax.dot_general(
        left, right, (((1,), (1,)), ((), ())), preferred_element_type=jnp.float32
    )


def attention_weights(attn_gain, w_qkv, w_attn_out):
    return (
        lax.all_gather(attn_gain, "dp", axis=0, tiled=True),
        lax.all_gather(w_qkv, "dp", axis=0, tiled=True),
        lax.all_gather(w_attn_out, "dp", axis=1, tiled=True),
    )


def feedforward_weights(mlp_gain, w_in, w_mlp_out):
    return (
        lax.all_gather(mlp_gain, "dp", axis=0, tiled=True),
        lax.all_gather(w_in, "dp", axis=0, tiled=True),
        lax.all_gather(w_mlp_out, "dp", axis=1, tiled=True),
    )


def attention_forward(queries, key_rows, value_rows):
    length, head_count, head_width = queries.shape
    block_size = min(query_block, length)
    score_scale = head_width ** (-0.5)
    blocks = queries.reshape(length // block_size, block_size, head_count, head_width)

    def one_block(block_rows):
        scores = (
            jnp.einsum("qhd,khd->hqk", block_rows, key_rows, preferred_element_type=jnp.float32)
            * score_scale
        )
        row_peak = jnp.max(scores, axis=-1, keepdims=True)
        exp_scores = jnp.exp(scores - row_peak)
        row_total = jnp.sum(exp_scores, axis=-1, keepdims=True)
        attn_probs = (exp_scores / row_total).astype(jnp.bfloat16)
        block_out = jnp.einsum(
            "hqk,khd->qhd", attn_probs, value_rows, preferred_element_type=jnp.float32
        )
        return (block_out.astype(jnp.bfloat16), (row_peak + jnp.log(row_total))[..., 0])

    outs, log_totals = lax.map(one_block, blocks)
    return (outs.reshape(length, head_count, head_width), log_totals)


def attention_backward(queries, key_rows, value_rows, attended, log_totals, grad_out):
    length, head_count, head_width = queries.shape
    block_size = min(query_block, length)
    nblocks = length // block_size
    score_scale = head_width ** (-0.5)

    def one_block(running, block_inputs):
        key_grad, value_grad = running
        block_rows, out_rows, grad_rows, lse_rows = block_inputs
        scores = (
            jnp.einsum("qhd,khd->hqk", block_rows, key_rows, preferred_element_type=jnp.float32)
            * score_scale
        )
        attn_probs = jnp.exp(scores - lse_rows[..., None])
        value_grad = value_grad + jnp.einsum(
            "hqk,qhd->khd",
            attn_probs.astype(jnp.bfloat16),
            grad_rows,
            preferred_element_type=jnp.float32,
        )
        dprobs = jnp.einsum(
            "qhd,khd->hqk", grad_rows, value_rows, preferred_element_type=jnp.float32
        )
        row_delta = jnp.sum(grad_rows.astype(jnp.float32) * out_rows.astype(jnp.float32), axis=-1).T
        dscores = (attn_probs * (dprobs - row_delta[..., None]) * score_scale).astype(jnp.bfloat16)
        query_grad = jnp.einsum(
            "hqk,khd->qhd", dscores, key_rows, preferred_element_type=jnp.float32
        )
        key_grad = key_grad + jnp.einsum(
            "hqk,qhd->khd", dscores, block_rows, preferred_element_type=jnp.float32
        )
        return ((key_grad, value_grad), query_grad)

    zero_grad = jnp.zeros((length, head_count, head_width), jnp.float32)
    shape_blocks = (nblocks, block_size, head_count, head_width)
    block_inputs = (
        queries.reshape(shape_blocks),
        attended.reshape(shape_blocks),
        grad_out.reshape(shape_blocks),
        log_totals,
    )
    (key_grad, value_grad), query_grad = lax.scan(one_block, (zero_grad, zero_grad), block_inputs)
    return (query_grad.reshape(length, head_count, head_width), key_grad, value_grad)


def shards(tokens, cotangent, attn_gain, w_qkv, w_attn_out, mlp_gain, w_in, w_mlp_out):
    gain_one, qkv_full, out_full = attention_weights(attn_gain, w_qkv, w_attn_out)
    gain_two, in_full, down_full = feedforward_weights(mlp_gain, w_in, w_mlp_out)
    model_width = tokens.shape[1]
    residual = tokens.astype(jnp.float32)
    normed_one, inverse_one = norm_stats(residual)
    first_in = (normed_one * gain_one.astype(jnp.float32)).astype(jnp.bfloat16)
    first_all = lax.all_gather(first_in, "mp", axis=0, tiled=True)
    length = first_all.shape[0]
    local_width = qkv_full.shape[2]
    head_count = local_width // HEAD_DIM
    cosine_table, sine_table = rotary_tables(length, HEAD_DIM)
    projected = jnp.dot(
        first_all,
        qkv_full.reshape(model_width, 3 * local_width),
        preferred_element_type=jnp.float32,
    )
    projected = projected.reshape(length, 3, head_count, HEAD_DIM)
    queries = apply_rotary(projected[:, 0], cosine_table, sine_table).astype(jnp.bfloat16)
    key_rows = apply_rotary(projected[:, 1], cosine_table, sine_table).astype(jnp.bfloat16)
    value_rows = projected[:, 2].astype(jnp.bfloat16)
    attended, log_totals = attention_forward(queries, key_rows, value_rows)
    attended_flat = attended.reshape(length, local_width)
    mixed_rows = residual + lax.psum_scatter(
        jnp.dot(attended_flat, out_full, preferred_element_type=jnp.float32),
        "mp",
        scatter_dimension=0,
        tiled=True,
    )
    normed_two, inverse_two = norm_stats(mixed_rows)
    second_in = (normed_two * gain_two.astype(jnp.float32)).astype(jnp.bfloat16)
    second_all = lax.all_gather(second_in, "mp", axis=0, tiled=True)
    unit_count = in_full.shape[2]
    lifted = jnp.dot(
        second_all, in_full.reshape(model_width, 2 * unit_count), preferred_element_type=jnp.float32
    )
    lifted = lifted.reshape(length, 2, unit_count)
    inputs = lifted[:, 0]
    gate_vals = lifted[:, 1]
    activated = gelu_exact(inputs)
    hidden = (activated * gate_vals).astype(jnp.bfloat16)
    output = mixed_rows + lax.psum_scatter(
        jnp.dot(hidden, down_full, preferred_element_type=jnp.float32).astype(jnp.bfloat16),
        "mp",
        scatter_dimension=0,
        tiled=True,
    ).astype(jnp.float32)
    gain_two, in_full, down_full = feedforward_weights(mlp_gain, w_in, w_mlp_out)
    gain_one, qkv_full, out_full = attention_weights(attn_gain, w_qkv, w_attn_out)
    cot_all = lax.all_gather(cotangent, "mp", axis=0, tiled=True)
    hidden_grad = times_transposed(cot_all, down_full)
    down_grad = contract_rows(hidden, cot_all)
    input_grad = hidden_grad * gate_vals * gelu_slope(inputs)
    gate_grad = hidden_grad * activated
    lifted_grad = (
        jnp.stack([input_grad, gate_grad], axis=1)
        .astype(jnp.bfloat16)
        .reshape(length, 2 * unit_count)
    )
    in_grad = contract_rows(second_all, lifted_grad).reshape(model_width, 2, unit_count)
    in_flat = in_full.reshape(model_width, 2 * unit_count)
    second_grad = lax.psum_scatter(
        times_transposed(lifted_grad, in_flat), "mp", scatter_dimension=0, tiled=True
    )
    back_two, gain_two_part = norm_backward(
        second_grad, normed_two, inverse_two, gain_two.astype(jnp.float32)
    )
    mixed_grad = cotangent.astype(jnp.float32) + back_two
    mixed_low = mixed_grad.astype(jnp.bfloat16)
    mixed_all = lax.all_gather(mixed_low, "mp", axis=0, tiled=True)
    attended_grad = (
        times_transposed(mixed_all, out_full)
        .astype(jnp.bfloat16)
        .reshape(length, head_count, HEAD_DIM)
    )
    out_grad = contract_rows(attended_flat, mixed_all)
    query_grad, key_grad, value_grad = attention_backward(
        queries, key_rows, value_rows, attended, log_totals, attended_grad
    )
    query_grad = undo_rotary(query_grad, cosine_table, sine_table)
    key_grad = undo_rotary(key_grad, cosine_table, sine_table)
    projected_grad = (
        jnp.stack([query_grad, key_grad, value_grad], axis=1)
        .astype(jnp.bfloat16)
        .reshape(length, 3 * local_width)
    )
    qkv_grad = contract_rows(first_all, projected_grad).reshape(model_width, 3, local_width)
    qkv_flat = qkv_full.reshape(model_width, 3 * local_width)
    first_grad = lax.psum_scatter(
        times_transposed(projected_grad, qkv_flat).astype(jnp.bfloat16),
        "mp",
        scatter_dimension=0,
        tiled=True,
    ).astype(jnp.float32)
    back_one, gain_one_part = norm_backward(
        first_grad, normed_one, inverse_one, gain_one.astype(jnp.float32)
    )
    tokens_grad = mixed_grad + back_one
    down_shard, in_shard, gain_two_shard, out_shard, qkv_shard, gain_one_shard = (
        lax.psum_scatter(down_grad, "dp", scatter_dimension=1, tiled=True),
        lax.psum_scatter(in_grad, "dp", scatter_dimension=0, tiled=True),
        lax.psum_scatter(gain_two_part, "dp", scatter_dimension=0, tiled=True),
        lax.psum_scatter(out_grad, "dp", scatter_dimension=1, tiled=True),
        lax.psum_scatter(qkv_grad, "dp", scatter_dimension=0, tiled=True),
        lax.psum_scatter(gain_one_part, "dp", scatter_dimension=0, tiled=True),
    )
    gain_one_grad, gain_two_grad = lax.psum((gain_one_shard, gain_two_shard), "mp")
    return (
        output,
        tokens_grad,
        gain_one_grad,
        qkv_shard,
        out_shard,
        gain_two_grad,
        in_shard,
        down_shard,
    )


def solution(mesh):
    in_specs = (
        P(("dp", "mp"), None),
        P(("dp", "mp"), None),
        P("dp"),
        P("dp", None, "mp"),
        P("mp", "dp"),
        P("dp"),
        P("dp", None, "mp"),
        P("mp", "dp"),
    )
    out_specs = (
        P(("dp", "mp"), None),
        P(("dp", "mp"), None),
        P("dp"),
        P("dp", None, "mp"),
        P("mp", "dp"),
        P("dp"),
        P("dp", None, "mp"),
        P("mp", "dp"),
    )
    return jax.shard_map(shards, mesh=mesh, in_specs=in_specs, out_specs=out_specs, check_vma=False)
```

profile of v0, /device:TPU:25, one launch (start us, length us, event | category | flops | bytes accessed | tf_op | source)
XLA Modules:
  0.0 583.5 jit_solution(15438715168269860549)
XLA Ops:
  7.2 1.0 convert_reduce_fusion
  8.3 1.1 fusion.38
  9.5 1.3 fusion.58
  13.1 13.3 %all-reduce.6 = (bf16[768]{0:T(1024)(128)(2,1)S(1)}, bf16[768]{0:T(1024)(128)(2,1)S(1)}) all-reduce(bf16[768]{0:T(1024)(128)(2,1)S(1)} %dynamic-update-slice, bf16[768]{0:T(1024)(128)(2,1)S(1)} %dynamic-update-slice.1), channel_id=1, replica_groups=mesh['dp'=8,'mp'=4] {'dp'}, use_global_device_ids=true, to_apply=%add | all-reduce | flops 1536 | bytes 6144
  27.5 1.0 copy.36
  28.8 26.5 %all_gather.39 = bf16[192,768]{0,1:T(8,128)(2,1)S(1)} all-gather(bf16[192,96]{0,1:T(8,128)(2,1)S(1)} %copy.39), channel_id=1, replica_groups=mesh['dp'=8,'mp'=4] {'dp'}, dimensions={1}, use_global_device_ids=true | all-gather | bytes 331776 | tf_op jit(solution)/shard_map/all_gather | solution.py:79
  55.2 1.2 fusion.34
  56.5 19.0 %all_gather.37 = bf16[512,768]{1,0:T(8,128)(2,1)S(1)} all-gather(bf16[128,768]{1,0:T(8,128)(2,1)S(1)} %fusion.34), channel_id=1, replica_groups=mesh['dp'=8,'mp'=4] {'mp'}, dimensions={0}, use_global_device_ids=true | all-gather | bytes 983040 | tf_op jit(solution)/shard_map/all_gather | solution.py:167
  75.5 34.7 %all_gather.38 = bf16[768,3,192]{2,1,0:T(4,128)(2,1)S(1)} all-gather(bf16[96,3,192]{2,1,0:T(4,128)(2,1)S(1)} %copy.36), channel_id=1, replica_groups=mesh['dp'=8,'mp'=4] {'dp'}, dimensions={0}, use_global_device_ids=true | all-gather | bytes 995328 | tf_op jit(solution)/shard_map/all_gather | solution.py:78
  110.2 2.1 copy.37
  112.3 1.8 fusion.13
  117.9 1.6 fusion.59
  121.6 29.2 %all_gather.42 = bf16[768,2,288]{2,0,1:T(8,128)(2,1)} all-gather(bf16[96,2,288]{2,0,1:T(8,128)(2,1)S(1)} %copy.40), channel_id=1, replica_groups=mesh['dp'=8,'mp'=4] {'dp'}, dimensions={0}, use_global_device_ids=true | all-gather | bytes 995328 | tf_op jit(solution)/shard_map/all_gather | solution.py:86
  150.8 2.3 copy.41
  153.0 27.4 %all_gather.43 = bf16[288,768]{0,1:T(8,128)(2,1)} all-gather(bf16[288,96]{0,1:T(8,128)(2,1)S(1)} %copy.42), channel_id=1, replica_groups=mesh['dp'=8,'mp'=4] {'dp'}, dimensions={1}, use_global_device_ids=true | all-gather | bytes 497664 | tf_op jit(solution)/shard_map/all_gather | solution.py:87
  180.5 22.8 %all_gather.44 = bf16[512,768]{1,0:T(8,128)(2,1)} all-gather(bf16[128,768]{1,0:T(8,128)(2,1)S(1)} %copy-done.26), channel_id=1, replica_groups=mesh['dp'=8,'mp'=4] {'mp'}, dimensions={0}, use_global_device_ids=true | all-gather | bytes 983040 | tf_op jit(solution)/shard_map/all_gather | solution.py:209
  203.3 1.2 fusion.57
  205.3 8.7 %all_gather.41 = bf16[512,768]{1,0:T(8,128)(2,1)S(1)} all-gather(bf16[128,768]{1,0:T(8,128)(2,1)S(1)} %multiply_convert_fusion.2), channel_id=1, replica_groups=mesh['dp'=8,'mp'=4] {'mp'}, dimensions={0}, use_global_device_ids=true | all-gather | bytes 983040 | tf_op jit(solution)/shard_map/all_gather | solution.py:191
  218.1 2.0 convolution_bitcast_fusion
  220.2 1.4 multiply_convert_fusion.1
  222.3 2.6 convolution_convert_fusion.1
  224.9 2.9 convolution_bitcast_fusion.1
  227.9 3.6 fusion.17
  232.3 17.4 %reduce-scatter.17.cloned.1.call-done = f32[128,768]{1,0:T(8,128)} async-done(((f32[512,768]{1,0:T(8,128)}), f32[128,768]{1,0:T(8,128)}) %reduce-scatter.17.cloned.1.call-update) | async-done | bytes 393232 | tf_op jit(solution)/shard_map/reduce_scatter | solution.py:221
  249.7 1.2 multiply_reduce_fusion.1
  251.5 24.0 %reduce-scatter.15.cloned.1.call-done = bf16[128,768]{1,0:T(8,128)(2,1)} async-done(((bf16[512,768]{1,0:T(8,128)(2,1)}), bf16[128,768]{1,0:T(8,128)(2,1)}) %reduce-scatter.15.cloned.1.call-update) | async-done | bytes 196624 | tf_op jit(solution)/shard_map/reduce_scatter | solution.py:201
  275.5 2.2 fusion.56
  277.6 8.9 %all_gather.45 = bf16[512,768]{1,0:T(8,128)(2,1)S(1)} all-gather(bf16[128,768]{1,0:T(8,128)(2,1)S(1)} %get-tuple-element.92), channel_id=1, replica_groups=mesh['dp'=8,'mp'=4] {'mp'}, dimensions={0}, use_global_device_ids=true | all-gather | bytes 983040 | tf_op jit(solution)/shard_map/all_gather | solution.py:229
  287.0 1.4 convolution_bitcast_fusion.2
  288.5 2.0 multiply_convert_fusion
  291.1 1.4 broadcast_multiply_fusion.1
  292.6 1.1 slice_negate_fusion.1
  293.7 1.1 slice_negate_fusion
  294.8 1.2 fusion.45
  297.2 1.7 convolution_convert_fusion
  299.0 2.3 fusion.15
  302.1 38.6 %reduce-scatter.27.cloned.1.call-done = f32[96,288]{1,0:T(8,128)} async-done(((f32[768,288]{1,0:T(8,128)}), f32[96,288]{1,0:T(8,128)}) %reduce-scatter.27.cloned.1.call-update) | async-done | bytes 110608
  340.6 1.7 copy.63
  342.3 70.1 %reduce-scatter.23.cloned.1.call-done = f32[96,2,288]{2,0,1:T(8,128)} async-done(((f32[768,2,288]{2,0,1:T(8,128)}), f32[96,2,288]{2,0,1:T(8,128)}) %reduce-scatter.23.cloned.1.call-update) | async-done | bytes 221200 | tf_op jit(solution)/shard_map/reduce_scatter | solution.py:260
  412.4 1.9 copy.49
  414.3 64.1 %reduce-scatter.25.cloned.1.call-done = f32[96,192]{1,0:T(8,128)} async-done(((f32[768,192]{1,0:T(8,128)}), f32[96,192]{1,0:T(8,128)}) %reduce-scatter.25.cloned.1.call-update) | async-done | bytes 73744
  478.4 1.6 copy.61
  480.0 26.0 %reduce-scatter.19.cloned.1.call-done = bf16[128,768]{1,0:T(8,128)(2,1)} async-done(((bf16[512,768]{1,0:T(8,128)(2,1)}), bf16[128,768]{1,0:T(8,128)(2,1)}) %reduce-scatter.19.cloned.1.call-update) | async-done | bytes 196624 | tf_op jit(solution)/shard_map/reduce_scatter | solution.py:248
  506.0 1.2 fusion.40
  507.2 14.1 %all-reduce.4 = (f32[768]{0:T(1024)S(1)}, f32[768]{0:T(1024)S(1)}) all-reduce(f32[768]{0:T(1024)S(1)} %get-tuple-element.83, f32[768]{0:T(1024)S(1)} %get-tuple-element.80), channel_id=6, replica_groups=mesh['dp'=8,'mp'=4] {'dp'}, use_global_device_ids=true, to_apply=%region_16.17.clone | all-reduce | flops 1536 | bytes 12288
  521.5 9.6 %all-reduce.5 = (f32[96]{0:T(128)}, f32[96]{0:T(128)}) all-reduce(f32[96]{0:T(128)S(1)} %dynamic-slice.5, f32[96]{0:T(128)S(1)} %dynamic-slice.7), channel_id=1, replica_groups=mesh['dp'=8,'mp'=4] {'mp'}, use_global_device_ids=true, to_apply=%region_17.18 | all-reduce | flops 192 | bytes 1536 | tf_op jit(solution)/shard_map/psum | solution.py:266
  531.1 1.9 fusion.37
  533.0 43.7 %reduce-scatter.21.cloned.1.call-done = f32[96,3,192]{2,0,1:T(8,128)} async-done(((f32[768,3,192]{2,0,1:T(8,128)}), f32[96,3,192]{2,0,1:T(8,128)}) %reduce-scatter.21.cloned.1.call-update) | async-done | bytes 221200 | tf_op jit(solution)/shard_map/reduce_scatter | solution.py:263
  (133 shorter events, 18.2 us)
Async XLA Ops:
  7.2 196.1 %reduce-scatter.13.cloned.1.call-start = ((), (), s32[]{:S(2)}) async-start(), calls=%async_computation.8 | async-start | bytes 1966080 | tf_op jit(solution)/shard_map/reduce_scatter | solution.py:183
  8.3 104.0 %copy-start.33 = (f32[128]{0:T(128)}, f32[128]{0:T(128)S(1)}, u32[]{:S(2)}) copy-start(f32[128]{0:T(128)S(1)} %broadcast_multiply_fusion.7) | copy-start | bytes 1540
  9.4 102.8 %copy-start.36 = (f32[128]{0:T(128)}, f32[128]{0:T(128)S(1)}, u32[]{:S(2)}) copy-start(f32[128]{0:T(128)S(1)} %add_rsqrt_fusion.1) | copy-start | bytes 1540
  26.5 85.8 %copy-start.29 = (f32[768]{0:T(1024)}, f32[768]{0:T(1024)S(1)}, u32[]{:S(2)}) copy-start(f32[768]{0:T(1024)S(1)} %convert_element_type.100) | copy-start | bytes 9220
  28.7 85.5 %copy-start.23 = (f32[512,64]{0,1:T(8,128)}, f32[512,64]{0,1:T(8,128)S(1)}, u32[]{:S(2)}) copy-start(f32[512,64]{0,1:T(8,128)S(1)} %get-tuple-element.115) | copy-start | bytes 393220
  28.8 85.5 %copy-start.24 = (f32[512,64]{0,1:T(8,128)}, f32[512,64]{0,1:T(8,128)S(1)}, u32[]{:S(2)}) copy-start(f32[512,64]{0,1:T(8,128)S(1)} %get-tuple-element.116) | copy-start | bytes 393220
  55.2 61.9 %copy-start.9 = (bf16[192,768]{0,1:T(8,128)(2,1)}, bf16[192,768]{0,1:T(8,128)(2,1)S(1)}, u32[]{:S(2)}) copy-start(bf16[192,768]{0,1:T(8,128)(2,1)S(1)} %all_gather.39) | copy-start | bytes 884740
  75.5 38.6 %copy-start.2 = (bf16[512,768]{1,0:T(8,128)(2,1)}, bf16[512,768]{1,0:T(8,128)(2,1)S(1)}, u32[]{:S(2)}) copy-start(bf16[512,768]{1,0:T(8,128)(2,1)S(1)} %all_gather.37) | copy-start | bytes 2359300
  114.1 2.3 copy-start
  114.5 0.7 copy-start.16
  114.5 1.4 copy-start.20
  116.4 0.8 copy-start.32
  117.2 0.7 copy-start.18
  119.5 61.0 %copy-start.26 = (bf16[128,768]{1,0:T(8,128)(2,1)S(1)}, bf16[128,768]{1,0:T(8,128)(2,1)}, u32[]{:S(2)}) copy-start(bf16[128,768]{1,0:T(8,128)(2,1)} %param.9) | copy-start | bytes 589828
  119.5 130.2 %reduce-scatter.17.cloned.1.call-start = ((), (), s32[]{:S(2)}) async-start(), calls=%async_computation.10 | async-start | bytes 1966080 | tf_op jit(solution)/shard_map/reduce_scatter | solution.py:221
  119.6 85.2 %copy-start.31 = (f32[768]{0:T(1024)}, f32[768]{0:T(1024)S(1)}, u32[]{:S(2)}) copy-start(f32[768]{0:T(1024)S(1)} %convert_element_type.108) | copy-start | bytes 9220
  203.3 11.7 %copy-start.8 = (bf16[768,2,288]{0,2,1:T(8,128)(2,1)S(1)}, bf16[768,2,288]{0,2,1:T(8,128)(2,1)}, u32[]{:S(2)}) copy-start(bf16[768,2,288]{0,2,1:T(8,128)(2,1)} %copy.41) | copy-start | bytes 2654212
  204.6 0.5 copy-start.35
  204.6 12.1 %copy-start.11 = (bf16[512,768]{1,0:T(8,128)(2,1)S(1)}, bf16[512,768]{1,0:T(8,128)(2,1)}, u32[]{:S(2)}) copy-start(bf16[512,768]{1,0:T(8,128)(2,1)} %all_gather.44) | copy-start | bytes 2359300
  204.6 12.1 %copy-start.15 = (bf16[288,768]{0,1:T(8,128)(2,1)S(1)}, bf16[288,768]{0,1:T(8,128)(2,1)}, u32[]{:S(2)}) copy-start(bf16[288,768]{0,1:T(8,128)(2,1)} %all_gather.43) | copy-start | bytes 1327108
  204.8 0.5 copy-start.38
  214.0 1.0 copy-start.4
  215.6 1.0 copy-start.6
  216.6 1.5 copy-start.5
  217.3 0.7 copy-start.27
  217.3 0.8 copy-start.28
  220.2 55.3 %reduce-scatter.15.cloned.1.call-start = ((), (), s32[]{:S(2)}) async-start(), calls=%async_computation.9 | async-start | bytes 983040 | tf_op jit(solution)/shard_map/reduce_scatter | solution.py:201
  221.6 0.7 copy-start.14
  224.9 115.7 %reduce-scatter.27.cloned.1.call-start = ((), (), s32[]{:S(2)}) async-start(), calls=%async_computation.15 | async-start | bytes 1327104
  227.9 184.5 %reduce-scatter.23.cloned.1.call-start = ((), (), s32[]{:S(2)}) async-start(), calls=%async_computation.13 | async-start | bytes 2654208 | tf_op jit(solution)/shard_map/reduce_scatter | solution.py:260
  231.5 246.8 %reduce-scatter.25.cloned.1.call-start = ((), (), s32[]{:S(2)}) async-start(), calls=%async_computation.14 | async-start | bytes 884736
  275.5 11.1 %copy-start.10 = (bf16[192,768]{0,1:T(8,128)(2,1)S(1)}, bf16[192,768]{0,1:T(8,128)(2,1)}, u32[]{:S(2)}) copy-start(bf16[192,768]{0,1:T(8,128)(2,1)} %copy-done.9) | copy-start | bytes 884740
  275.5 11.5 %copy-start.19 = (bf16[3,64,512]{2,1,0:T(8,128)(2,1)S(1)}, bf16[3,64,512]{2,1,0:T(8,128)(2,1)}, u32[]{:S(2)}) copy-start(bf16[3,64,512]{2,1,0:T(8,128)(2,1)} %copy-done.18) | copy-start | bytes 589828
  286.9 1.5 copy-start.12
  288.5 2.0 copy-start.17
  288.5 2.6 copy-start.21
  288.5 2.6 copy-start.25
  292.5 213.4 %reduce-scatter.19.cloned.1.call-start = ((), (), s32[]{:S(2)}) async-start(), calls=%async_computation.11 | async-start | bytes 983040 | tf_op jit(solution)/shard_map/reduce_scatter | solution.py:248
  292.6 3.4 copy-start.13
  296.0 1.2 copy-start.7
  296.7 2.3 copy-start.3
  299.0 277.7 %reduce-scatter.21.cloned.1.call-start = ((), (), s32[]{:S(2)}) async-start(), calls=%async_computation.12 | async-start | bytes 2654208 | tf_op jit(solution)/shard_map/reduce_scatter | solution.py:263
  301.3 204.7 %copy-start.1 = (bf16[128,768]{1,0:T(8,128)(2,1)S(1)}, bf16[128,768]{1,0:T(8,128)(2,1)}, u32[]{:S(2)}) copy-start(bf16[128,768]{1,0:T(8,128)(2,1)} %param.8) | copy-start | bytes 589828
  301.3 204.7 %copy-start.30 = (f32[768]{0:T(1024)S(1)}, f32[768]{0:T(1024)}, u32[]{:S(2)}) copy-start(f32[768]{0:T(1024)} %copy-done.29) | copy-start | bytes 9220
  301.3 204.7 %copy-start.34 = (f32[128]{0:T(128)S(1)}, f32[128]{0:T(128)}, u32[]{:S(2)}) copy-start(f32[128]{0:T(128)} %copy-done.33) | copy-start | bytes 1540
  301.3 204.7 %copy-start.37 = (f32[128]{0:T(128)S(1)}, f32[128]{0:T(128)}, u32[]{:S(2)}) copy-start(f32[128]{0:T(128)} %copy-done.36) | copy-start | bytes 1540
  301.3 229.8 %copy-start.22 = (f32[128,768]{1,0:T(8,128)S(1)}, f32[128,768]{1,0:T(8,128)}, u32[]{:S(2)}) copy-start(f32[128,768]{1,0:T(8,128)} %get-tuple-element.93) | copy-start | bytes 1179652
Sparse Core Ops, SparseCore 0:
  119.6 30.9 reduce-scatter.12
  220.3 29.3 reduce-scatter.16
  252.2 23.1 reduce-scatter.14
  278.7 61.8 reduce-scatter.26
  344.0 68.3 reduce-scatter.22
  415.6 62.7 reduce-scatter.24
  480.9 25.0 reduce-scatter.18
  510.0 66.5 reduce-scatter.20
where the time goes:
time: 590 us; the launch traced here: 583 us
  waiting for transfers between devices  284 us (48%)
  blocking collectives  214 us (36%)
  matrix products  27.7 us (5%)
  local copies, waits for them, and re-layouts  22.4 us (4%)
  other arithmetic  18.7 us (3%)
  between operations  16.1 us (3%)
    unnamed x10, waiting for transfers between devices  103 us
    reduce_scatter x1, waiting for transfers between devices, shards(): lax.psum_scatter(in_grad, 'dp', scatter_dimension=0, tiled=True)  70.1 us
    reduce_scatter x1, waiting for transfers between devices, shards(): lax.psum_scatter(qkv_grad, 'dp', scatter_dimension=0, tiled=True)  43.7 us
    all_gather x1, blocking collectives, attention_weights(): lax.all_gather(w_qkv, 'dp', axis=0, tiled=True)  34.7 us
    all_gather x1, blocking collectives, feedforward_weights(): lax.all_gather(w_in, 'dp', axis=0, tiled=True)  29.2 us
    unnamed x2, blocking collectives  27.5 us
    all_gather x1, blocking collectives, feedforward_weights(): lax.all_gather(w_mlp_out, 'dp', axis=1, tiled=True)  27.4 us
    all_gather x1, blocking collectives, attention_weights(): lax.all_gather(w_attn_out, 'dp', axis=1, tiled=True)  26.5 us
  transfers between devices with their start and end apart: 8, of which 7 were waited for; matrix products, arithmetic and copies ran while one was open for 7% of the time, Pallas kernels for 0%

commit v1 on v0

--- a/solution.py
+++ b/solution.py
@@ -1,7 +1,17 @@
+import functools
+
 import jax
 import jax.numpy as jnp
+import numpy as np
 from jax import lax
+from jax.experimental import pallas as pl
+from jax.experimental.pallas import tpu as pltpu
 from jax.sharding import PartitionSpec as P
+
+MESH = pl.DeviceIdType.MESH
+PAIR = 2
+BF = jnp.bfloat16
+F32 = jnp.float32
 
 HEAD_DIM = 64
 
@@ -276,6 +286,492 @@
     )
 
 
+def nn(left, right):
+    return lax.dot_general(left, right, (((1,), (0,)), ((), ())), preferred_element_type=F32)
+
+
+def nt(left, right):
+    return lax.dot_general(left, right, (((1,), (1,)), ((), ())), preferred_element_type=F32)
+
+
+def tn(left, right):
+    return lax.dot_general(left, right, (((0,), (0,)), ((), ())), preferred_element_type=F32)
+
+
+def erf(x):
+    return lax.erf(x)
+
+
+def swap_halves(tile):
+    lane = lax.broadcasted_iota(jnp.int32, tile.shape, 1)
+    half = HEAD_DIM // 2
+    back = pltpu.roll(tile, tile.shape[1] - half, 1)
+    ahead = pltpu.roll(tile, half, 1)
+    return jnp.where(lax.rem(lane, HEAD_DIM) < half, back, ahead)
+
+
+def layer_kernel(
+    ndp, heads,
+    tok, cot, gpad, gcol, wq, wo, wi, wd, cos_t, sin_t,
+    out_o, tg_o, gg_o, dq_o, do_o, di_o, dd_o,
+    gains, wqf, wof, wif, wdf,
+    x1, x2, xc, x3, xt1, xt2, xtc, xt3,
+    qk, vb, att, pbuf, hid, actb, gateb, slopeb, lg, pg, gatt, dqs, dks, dvs,
+    xh1, xh2, mixed, mgrad,
+    rs_sc, rs_rc, rs_sy, rs_ry, rs_own,
+    gsq, grq, gzq, gyq, gwq,
+    gso, gro, gzo, gyo, gwo,
+    gsi, gri, gzi, gyi, gwi,
+    gsd, grd, gzd, gyd, gwd,
+    ggs, ggr,
+    send_sem, recv_sem,
+):
+    rows, width = tok.shape
+    nmp = x1.shape[0]
+    length = nmp * rows
+    na = ndp // PAIR
+    dp = lax.axis_index("dp")
+    mp = lax.axis_index("mp")
+    za = dp // PAIR
+    zb = lax.rem(dp, PAIR)
+    core = lax.rem(mp, 2)
+    ypos = mp // 2
+    mate = mp + 1 - 2 * core
+    ypeer = mp + 2 - 4 * ypos
+    diag = mate + 2 - 4 * ypos
+    xpeer = za * PAIR + (1 - zb)
+    local_width = heads * HEAD_DIM
+    units = hid.shape[1]
+    shard = wq.shape[0]
+
+    def at_dp(d):
+        return {"dp": d, "mp": mp}
+
+    def at_mp(m):
+        return {"dp": dp, "mp": m}
+
+    counter = [0]
+    sends = []
+
+    def slot():
+        counter[0] += 1
+        return counter[0] - 1
+
+    def put(src, dst, sem, dev):
+        copy = pltpu.make_async_remote_copy(
+            src_ref=src, dst_ref=dst, send_sem=send_sem.at[sem], recv_sem=recv_sem.at[sem],
+            device_id=dev, device_id_type=MESH,
+        )
+        copy.start()
+        sends.append(copy)
+
+    def got(buf, sem):
+        pltpu.make_async_remote_copy(
+            src_ref=buf, dst_ref=buf, send_sem=send_sem.at[sem], recv_sem=recv_sem.at[sem],
+            device_id=at_mp(mate), device_id_type=MESH,
+        ).wait_recv()
+
+    barrier = pltpu.get_barrier_semaphore()
+    for k in range(1, ndp):
+        pl.semaphore_signal(barrier, inc=1, device_id=at_dp(lax.rem(dp + k, ndp)), device_id_type=MESH)
+    for other in (mate, ypeer, diag):
+        pl.semaphore_signal(barrier, inc=1, device_id=at_mp(other), device_id_type=MESH)
+    pl.semaphore_wait(barrier, ndp - 1 + 3)
+
+    gain_slots = [slot() for _ in range(ndp - 1)]
+    for k in range(1, ndp):
+        put(gpad, gains.at[dp], gain_slots[k - 1], at_dp(lax.rem(dp + k, ndp)))
+
+    def gather_start(src, full):
+        zs = [slot() for _ in range(na)]
+        xs = [slot() for _ in range(na)]
+        for k in range(1, na):
+            put(src, full.at[dp], zs[k], at_dp(lax.rem(za + k, na) * PAIR + zb))
+        put(src, full.at[dp], xs[0], at_dp(xpeer))
+        full[dp] = src[...]
+        return (full, zs, xs)
+
+    def gather_forward(state):
+        full, zs, xs = state
+        for k in range(1, na):
+            source = lax.rem(za + na - k, na) * PAIR + zb
+            got(full.at[source], zs[k])
+            put(full.at[source], full.at[source], xs[k], at_dp(xpeer))
+
+    def gather_end(state):
+        full, zs, xs = state
+        for k in range(na):
+            source = lax.rem(za + na - k, na) * PAIR + (1 - zb)
+            got(full.at[source], xs[k])
+
+    def spread_start(buf):
+        sems = [slot() for _ in range(3)]
+        put(buf.at[mp], buf.at[mp], sems[0], at_mp(ypeer))
+        put(buf.at[mp], buf.at[mp], sems[1], at_mp(mate))
+        return (buf, sems)
+
+    def spread_forward(state):
+        buf, sems = state
+        got(buf.at[ypeer], sems[0])
+        put(buf.at[ypeer], buf.at[ypeer], sems[2], at_mp(mate))
+        got(buf.at[mate], sems[1])
+
+    def spread_end(state):
+        buf, sems = state
+        got(buf.at[diag], sems[2])
+
+    def scatter_sum(i, part):
+        s0, s1, s2 = slot(), slot(), slot()
+        far_mate = 2 * (1 - ypos) + (1 - core)
+        rs_sc[i, 0] = part(far_mate).astype(BF)
+        put(rs_sc.at[i, 0], rs_rc.at[i, 0], s0, at_mp(mate))
+        rs_sc[i, 1] = part(mate).astype(BF)
+        put(rs_sc.at[i, 1], rs_rc.at[i, 1], s1, at_mp(mate))
+        far = part(ypeer)
+        got(rs_rc.at[i, 0], s0)
+        rs_sy[i] = (far + rs_rc[i, 0].astype(F32)).astype(BF)
+        put(rs_sy.at[i], rs_ry.at[i], s2, at_mp(ypeer))
+        rs_own[i] = part(mp)
+        return (i, s1, s2)
+
+    def scatter_end(state):
+        i, s1, s2 = state
+        got(rs_rc.at[i, 1], s1)
+        near = rs_own[i] + rs_rc[i, 1].astype(F32)
+        got(rs_ry.at[i], s2)
+        return near + rs_ry[i].astype(F32)
+
+    def norm(vals):
+        centered = vals - jnp.mean(vals, axis=-1, keepdims=True)
+        inv = lax.rsqrt(jnp.mean(centered * centered, axis=-1, keepdims=True) + norm_eps)
+        return centered * inv, inv
+
+    def norm_back(grad, normed, inv, gain):
+        scaled = grad * gain
+        return inv * (
+            scaled
+            - jnp.mean(scaled, axis=-1, keepdims=True)
+            - normed * jnp.mean(scaled * normed, axis=-1, keepdims=True)
+        )
+
+    def turn(buf, dst):
+        @pl.loop(0, nmp)
+        def _(r):
+            cols = pl.ds(pl.multiple_of(r * rows, rows), rows)
+            flipped = buf[r].T
+            dst[:, :, :, cols] = flipped.reshape(na, PAIR, shard, rows)
+
+    def grad_start(xt, right, gs, gr, gw):
+        sems = [slot() for _ in range(na)]
+        cols = right.shape[1]
+        part = nn(xt[:, 1 - zb].reshape(na * shard, length), right)
+        gs[...] = part.astype(BF).reshape(na, shard, cols)
+        for k in [*range(1, na), 0]:
+            a = lax.rem(za + k, na)
+            put(gs.at[a], gr.at[a], sems[k], at_dp(xpeer))
+        gw[...] = nn(xt[:, zb].reshape(na * shard, length), right).reshape(na, shard, cols)
+        return (sems, gr, gw)
+
+    def grad_middle(state, gz, gy):
+        sems, gr, gw = state
+        zs = [slot() for _ in range(na)]
+        for k in range(1, na):
+            a = lax.rem(za + k, na)
+            got(gr.at[a], sems[k])
+            gz[k] = (gw[a] + gr[a].astype(F32)).astype(BF)
+            put(gz.at[k], gy.at[k], zs[k], at_dp(a * PAIR + zb))
+        got(gr.at[za], sems[0])
+        return (zs, gr, gw, gy)
+
+    def grad_end(state):
+        zs, gr, gw, gy = state
+        total = gw[za] + gr[za].astype(F32)
+        for k in range(1, na):
+            got(gy.at[k], zs[k])
+            total = total + gy[k].astype(F32)
+        return total
+
+    def tiles(count):
+        return [slice(i * 128, (i + 1) * 128) for i in range(count)]
+
+    ag_q = gather_start(wq, wqf)
+    gains[dp] = gpad[...]
+    for k in range(1, ndp):
+        source = lax.rem(dp + ndp - k, ndp)
+        got(gains.at[source], gain_slots[k - 1])
+    gain_all = gains[0]
+    for k in range(1, ndp):
+        gain_all = gain_all + gains[k]
+    gain_one = gain_all[:, :width]
+    gain_two = gain_all[:, width:]
+
+    residual = tok[...].astype(F32)
+    normed_one, inv_one = norm(residual)
+    xh1[...] = normed_one
+    x1[mp] = (normed_one * gain_one).astype(BF)
+    sp1 = spread_start(x1)
+    ag_o = gather_start(wo, wof)
+    spread_forward(sp1)
+    xc[mp] = cot[...]
+    spc = spread_start(xc)
+    gather_forward(ag_q)
+    ag_i = gather_start(wi, wif)
+    ag_d = gather_start(wd, wdf)
+    spread_end(sp1)
+    spread_forward(spc)
+    spread_end(spc)
+    turn(x1, xt1)
+    turn(xc, xtc)
+    gather_end(ag_q)
+
+    @pl.loop(0, nmp)
+    def _(r):
+        at = pl.ds(pl.multiple_of(r * rows, rows), rows)
+        proj = nn(x1[r], wqf[...].reshape(width, 3 * local_width))
+        for t in tiles(2 * local_width // 128):
+            u = proj[:, t]
+            qk[at, t] = (u * cos_t[at, :] + swap_halves(u) * sin_t[at, :]).astype(BF)
+        vb[at, :] = proj[:, 2 * local_width :].astype(BF)
+
+    gather_forward(ag_o)
+    scale = HEAD_DIM ** (-0.5)
+
+    def head(ref, h, at=slice(None)):
+        return ref[at, h * HEAD_DIM : (h + 1) * HEAD_DIM]
+
+    @pl.loop(0, nmp)
+    def _(r):
+        at = pl.ds(pl.multiple_of(r * rows, rows), rows)
+        outs = []
+        for h in range(heads):
+            scores = nt(head(qk, h, at), head(qk, heads + h)) * scale
+            peak = jnp.max(scores, axis=-1, keepdims=True)
+            e = jnp.exp(scores - peak)
+            probs = e / jnp.sum(e, axis=-1, keepdims=True)
+            pbuf[h, at, :] = probs
+            outs.append(nn(probs.astype(BF), head(vb, h)))
+        att[at, :] = jnp.concatenate(outs, axis=1).astype(BF)
+
+    gather_end(ag_o)
+
+    def chunk(r):
+        return pl.ds(pl.multiple_of(r * rows, rows), rows)
+
+    def attn_part(r):
+        return nt(att[chunk(r), :], wof[...].reshape(width, local_width))
+
+    rs_a = scatter_sum(0, attn_part)
+    gather_forward(ag_i)
+    gather_forward(ag_d)
+    mixed[...] = residual + scatter_end(rs_a)
+    normed_two, inv_two = norm(mixed[...])
+    xh2[...] = normed_two
+    x2[mp] = (normed_two * gain_two).astype(BF)
+    sp2 = spread_start(x2)
+    gather_end(ag_i)
+    gather_end(ag_d)
+    spread_forward(sp2)
+    spread_end(sp2)
+
+    @pl.loop(0, nmp)
+    def _(r):
+        at = chunk(r)
+        lifted = nn(x2[r], wif[...].reshape(width, 2 * units))
+        u = lifted[:, :units]
+        gate = lifted[:, units:]
+        cdf = 0.5 * (1.0 + erf(u * 0.7071067811865476))
+        act = u * cdf
+        slope = cdf + u * jnp.exp(-0.5 * u * u) * 0.3989422804014327
+        hid[at, :] = (act * gate).astype(BF)
+        hgrad = nn(xc[r], wdf[...].reshape(width, units))
+        lg[at, :] = jnp.concatenate([hgrad * gate * slope, hgrad * act], axis=1).astype(BF)
+
+    def in_part(r):
+        return nt(lg[chunk(r), :], wif[...].reshape(width, 2 * units))
+
+    def down_part(r):
+        return nt(hid[chunk(r), :], wdf[...].reshape(width, units))
+
+    rs_g = scatter_sum(1, in_part)
+    g_d = grad_start(xtc, hid[...], gsd, grd, gwd)
+    back_two = norm_back(scatter_end(rs_g), xh2[...], inv_two, gain_two)
+    mgrad[...] = cot[...].astype(F32) + back_two
+    x3[mp] = mgrad[...].astype(BF)
+    sp3 = spread_start(x3)
+    turn(x2, xt2)
+    spread_forward(sp3)
+    g_d = grad_middle(g_d, gzd, gyd)
+    g_i = grad_start(xt2, lg[...], gsi, gri, gwi)
+    spread_end(sp3)
+
+    dks[...] = jnp.zeros_like(dks)
+    dvs[...] = jnp.zeros_like(dvs)
+
+    @pl.loop(0, nmp)
+    def _(r):
+        at = chunk(r)
+        agrad = nn(x3[r], wof[...].reshape(width, local_width)).astype(BF)
+        out_rows = att[at, :]
+        for h in range(heads):
+            g = agrad[:, h * HEAD_DIM : (h + 1) * HEAD_DIM]
+            o = out_rows[:, h * HEAD_DIM : (h + 1) * HEAD_DIM]
+            probs = pbuf[h, at, :]
+            dvs[h] += tn(probs.astype(BF), g)
+            dprobs = nt(g, head(vb, h))
+            delta = jnp.sum(g.astype(F32) * o.astype(F32), axis=-1, keepdims=True)
+            ds = (probs * (dprobs - delta) * scale).astype(BF)
+            dqs[h, at, :] = nn(ds, head(qk, heads + h))
+            dks[h] += tn(ds, head(qk, h, at))
+
+    @pl.loop(0, nmp)
+    def _(r):
+        at = chunk(r)
+        both = jnp.concatenate(
+            [dqs[h, at, :] for h in range(heads)] + [dks[h, at, :] for h in range(heads)], axis=1
+        )
+        for t in tiles(2 * local_width // 128):
+            u = both[:, t]
+            pg[at, t] = (u * cos_t[at, :] - swap_halves(u) * sin_t[at, :]).astype(BF)
+        pg[at, 2 * local_width :] = jnp.concatenate(
+            [dvs[h, at, :] for h in range(heads)], axis=1
+        ).astype(BF)
+
+    g_q = grad_start(xt1, pg[...], gsq, grq, gwq)
+
+    def qkv_part(r):
+        return nt(pg[chunk(r), :], wqf[...].reshape(width, 3 * local_width))
+
+    rs_f = scatter_sum(2, qkv_part)
+    g_q = grad_middle(g_q, gzq, gyq)
+    g_i = grad_middle(g_i, gzi, gyi)
+    rs_o = scatter_sum(3, down_part)
+    turn(x3, xt3)
+    g_o = grad_start(xt3, att[...], gso, gro, gwo)
+    back_one = norm_back(scatter_end(rs_f), xh1[...], inv_one, gain_one)
+    tg_o[...] = mgrad[...] + back_one
+    out_o[...] = mixed[...] + scatter_end(rs_o)
+    g_o = grad_middle(g_o, gzo, gyo)
+    dd_o[...] = grad_end(g_d)
+    in_grad = grad_end(g_i)
+    di_o[...] = in_grad
+    qkv_grad = grad_end(g_q)
+    dq_o[...] = qkv_grad
+    sum_one = jnp.sum(qkv_grad * wq[...].astype(F32), axis=-1, keepdims=True)
+    sum_two = jnp.sum(in_grad * wi[...].astype(F32), axis=-1, keepdims=True)
+    lane = lax.broadcasted_iota(jnp.int32, gcol.shape, 1)
+    ggs[...] = jnp.where(lane < 64, sum_one, sum_two) / gcol[...]
+    gain_sems = [slot() for _ in range(3)]
+    for k, other in enumerate((ypeer, mate, diag)):
+        put(ggs, ggr.at[k], gain_sems[k], at_mp(other))
+    do_o[...] = grad_end(g_o)
+    total = ggs[...]
+    for k in range(3):
+        got(ggr.at[k], gain_sems[k])
+        total = total + ggr[k]
+    gg_o[...] = total
+    for copy in sends:
+        copy.wait_send()
+
+
+def fused_shards(tokens, cotangent, attn_gain, w_qkv, w_attn_out, mlp_gain, w_in, w_mlp_out):
+    ndp = lax.axis_size("dp")
+    nmp = lax.axis_size("mp")
+    rows, width = tokens.shape
+    shard = w_qkv.shape[0]
+    lw = w_qkv.shape[2]
+    units = w_in.shape[2]
+    heads = lw // HEAD_DIM
+    length = rows * nmp
+    na = ndp // PAIR
+    place = lax.axis_index("dp") * shard
+    pad = jnp.zeros((2, width), F32)
+    pad = lax.dynamic_update_slice(
+        pad, jnp.stack([attn_gain, mlp_gain]).astype(F32), (0, place)
+    ).reshape(1, 2 * width)
+    gcol = jnp.concatenate(
+        [
+            jnp.broadcast_to(attn_gain.astype(F32)[:, None], (shard, 64)),
+            jnp.broadcast_to(mlp_gain.astype(F32)[:, None], (shard, 64)),
+        ],
+        axis=1,
+    )
+    half = HEAD_DIM // 2
+    freqs = rope_base ** (-(np.arange(half, dtype=np.float32) * np.float32(2.0) / HEAD_DIM))
+    angles = np.arange(length, dtype=np.float32)[:, None] * freqs.astype(np.float32)[None, :]
+    cos_t = np.tile(np.cos(angles).astype(np.float32), (1, 128 // half))
+    sin = np.sin(angles).astype(np.float32)
+    sin_t = np.tile(np.concatenate([-sin, sin], axis=1), (1, 128 // HEAD_DIM))
+
+    def buf(shape, dtype=BF):
+        return pltpu.VMEM(shape, dtype)
+
+    def grad_bufs(cols):
+        return [
+            buf((na, shard, cols)), buf((na, shard, cols)), buf((na, shard, cols)),
+            buf((na, shard, cols)), buf((na, shard, cols), F32),
+        ]
+
+    nsem = 7 + 8 * na + 3 * 4 + 3 * 4 + 8 * na + 3 + 8
+    scratch = [
+        buf((ndp, 1, 2 * width), F32),
+        buf((ndp, shard, 3 * lw)), buf((ndp, shard, lw)),
+        buf((ndp, shard, 2 * units)), buf((ndp, shard, units)),
+        *[buf((nmp, rows, width)) for _ in range(4)],
+        *[buf((na, PAIR, shard, length)) for _ in range(4)],
+        buf((length, 2 * lw)), buf((length, lw)), buf((length, lw)),
+        buf((heads, length, length), F32), buf((length, units)),
+        buf((8, 128)), buf((8, 128)), buf((8, 128)),
+        buf((length, 2 * units)), buf((length, 3 * lw)), buf((8, 128)),
+        *[buf((heads, length, HEAD_DIM), F32) for _ in range(3)],
+        *[buf((rows, width), F32) for _ in range(4)],
+        buf((4, 2, rows, width)), buf((4, 2, rows, width)),
+        buf((4, rows, width)), buf((4, rows, width)), buf((4, rows, width), F32),
+        *grad_bufs(3 * lw), *grad_bufs(lw), *grad_bufs(2 * units), *grad_bufs(units),
+        buf((shard, 128), F32), buf((3, shard, 128), F32),
+        pltpu.SemaphoreType.DMA((nsem,)), pltpu.SemaphoreType.DMA((nsem,)),
+    ]
+    vmem = pl.BlockSpec(memory_space=pltpu.VMEM)
+    shapes = [
+        (rows, width), (rows, width), (shard, 128), (shard, 3 * lw), (shard, lw),
+        (shard, 2 * units), (shard, units),
+    ]
+    out, tg, gg, dq, do, di, dd = pl.pallas_call(
+        functools.partial(layer_kernel, ndp, heads),
+        out_shape=[jax.ShapeDtypeStruct(s, F32) for s in shapes],
+        in_specs=[vmem] * 10,
+        out_specs=[vmem] * 7,
+        scratch_shapes=scratch,
+        compiler_params=pltpu.CompilerParams(
+            collective_id=0, has_side_effects=True, vmem_limit_bytes=60 * 1024 * 1024
+        ),
+    )(
+        tokens, cotangent, pad.reshape(1, 2 * width), gcol,
+        w_qkv.reshape(shard, 3 * lw), w_attn_out.T,
+        w_in.reshape(shard, 2 * units), w_mlp_out.T,
+        jnp.asarray(cos_t), jnp.asarray(sin_t),
+    )
+    return (
+        out, tg, gg[:, 0], dq.reshape(shard, 3, lw), do.T, gg[:, 64],
+        di.reshape(shard, 2, units), dd.T,
+    )
+
+
+def choose(tokens, cotangent, attn_gain, w_qkv, w_attn_out, mlp_gain, w_in, w_mlp_out):
+    ndp = lax.axis_size("dp")
+    shard = w_qkv.shape[0]
+    fits = (
+        lax.axis_size("mp") == 4
+        and ndp % PAIR == 0
+        and shard % 16 == 0
+        and w_mlp_out.shape[1] == shard
+        and tokens.shape[0] % 128 == 0
+        and tokens.shape[0] <= 128
+        and 2 * w_qkv.shape[2] % 128 == 0
+    )
+    form = fused_shards if fits else shards
+    return form(tokens, cotangent, attn_gain, w_qkv, w_attn_out, mlp_gain, w_in, w_mlp_out)
+
+
 def solution(mesh):
     in_specs = (
         P(("dp", "mp"), None),
@@ -297,4 +793,4 @@
         P("dp", None, "mp"),
         P("mp", "dp"),
     )
-    return jax.shard_map(shards, mesh=mesh, in_specs=in_specs, out_specs=out_specs, check_vma=False)
+    return jax.shard_map(choose, mesh=mesh, in_specs=in_specs, out_specs=out_specs, check_vma=False)

time: 590 us -> 132 us (0.22)
  waiting for transfers between devices: 284 us -> 0 us
  blocking collectives: 214 us -> 0 us
  Pallas kernels: 0 us -> 114 us
  matrix products: 27.7 us -> 0 us
  other arithmetic: 18.7 us -> 0.73 us
  between operations: 16.1 us -> 0.69 us
  local copies, waits for them, and re-layouts: 22.4 us -> 14.1 us
    reduce_scatter x6 -> x0, waiting for transfers between devices: 181 us -> none  [the longest x1 70.1 us: shards(): lax.psum_scatter(in_grad, 'dp', scatter_dimension=0, tiled=True)]
    all_gather x8 -> x0, blocking collectives: 177 us -> none  [the longest x1 34.7 us: attention_weights(): lax.all_gather(w_qkv, 'dp', axis=0, tiled=True)]
    pallas_call x0 -> x1, Pallas kernels: none -> 114 us  [fused_shards(): pl.pallas_call(functools.partial(layer_kernel, ndp, heads), out_shape=[ja...]
    unnamed x10 -> x0, waiting for transfers between devices: 103 us -> none
    unnamed x2 -> x0, blocking collectives: 27.5 us -> none
    dot_general x16 -> x0, matrix products: 23.4 us -> none  [the longest x2 5.85 us: contract_rows(): lax.dot_general(left, right, (((0,), (0,)), ((), ())), preferred_element_...]
    psum x1 -> x0, blocking collectives: 9.62 us -> none  [shards(): lax.psum((gain_one_shard, gain_two_shard), 'mp')]
    unnamed x92 -> x29, local copies, waits for them, and re-layouts: 18 us -> 8.44 us
  transfers between devices with their start and end apart: 8 -> 0, of which waited for: 7 -> 0; matrix products, arithmetic and copies ran while one was open for 7% -> 0% of each run, Pallas kernels for 0% -> 0%
where the time goes in v1:
time: 132 us; the launch traced here: 130 us
  Pallas kernels  114 us (86%)
  local copies, waits for them, and re-layouts  14.1 us (11%)
    pallas_call x1, Pallas kernels, fused_shards(): pl.pallas_call(functools.partial(layer_kernel, ndp, heads), out_shape=[ja...  114 us
    unnamed x29, local copies, waits for them, and re-layouts  8.44 us

profile of v1, /device:TPU:25, one launch (start us, length us, event | category | flops | bytes accessed | tf_op | source)
XLA Modules:
  0.0 129.9 jit_solution(2931821612834150177)
XLA Ops:
  0.6 0.0 copy-start.8
  0.6 0.0 copy-start.9
  0.7 0.6 copy-done.8
  1.3 0.0 copy-done.9
  1.3 0.3 dynamic_update_slice.3
  1.6 0.6 copy.32
  2.2 1.1 copy.24
  3.3 0.8 copy.27.wq
  4.1 0.0 copy-start.3
  4.1 0.1 broadcast_in_dim.7
  4.1 0.1 broadcast_in_dim.8
  4.2 0.7 pad_maximum_fusion.gcol
  4.9 0.0 copy-done.3
  5.0 0.0 copy-start.6
  5.0 0.8 reshape.35.wi
  5.8 0.1 copy-done.6
  5.9 0.0 copy-start.7
  5.9 0.7 copy.26
  6.6 0.1 copy-done.7
  6.7 0.7 copy.25
  7.4 114.4 %shard_map.161 = (f32[128,768]{1,0:T(8,128)}, f32[128,768]{1,0:T(8,128)}, f32[96,128]{1,0:T(8,128)}, f32[96,576]{1,0:T(8,128)}, f32[96,192]{1,0:T(8,128)}, /*index=5*/f32[96,576]{1,0:T(8,128)}, f32[96,288]{1,0:T(8,128)}) custom-call(bf16[128,768]{1,0:T(8,128)(2,1)} %tok.1, bf16[128,768]{1,0:T(8,128)(2,1)} %cot.1, f32[1,1536]{1,0:T(1,128)} %bitcast.17, ...), custom_call_target="tpu_custom_call" | custom-call | tf_op jit(solution)/shard_map/pallas_call | solution.py:738
  121.8 1.6 %slice_reduce_fusion = (f32[96]{0:T(128)}, f32[96]{0:T(128)}) fusion(f32[96,128]{1,0:T(8,128)} %get-tuple-element.17), kind=kLoop, calls=%fused_computation.1 | loop fusion | bytes 1536 | tf_op jit(solution)/shard_map/slice | solution.py:754
  123.4 1.1 copy.28
  124.5 0.0 copy-start.2
  124.5 0.9 copy.29
  125.4 0.1 copy-done.2
  125.5 0.0 copy-start.4
  125.5 0.0 copy-start.1
  125.5 0.9 reshape.37
  126.4 0.0 copy-done.4
  126.4 0.0 copy-start.5
  126.4 0.8 copy.31
  127.2 0.1 copy-done.5
  127.3 0.7 copy.30
  128.0 0.0 copy-done.1
  128.0 0.0 copy-start
  128.1 0.7 copy.36
  128.8 0.4 copy-done
  129.2 0.7 copy.37
  (2 shorter events, 0.0 us)
Async XLA Ops:
  0.6 0.7 copy-start.8
  0.6 0.7 copy-start.9
  4.1 0.9 copy-start.3
  5.0 0.9 copy-start.6
  5.9 0.8 copy-start.7
  124.5 0.9 copy-start.2
  125.5 1.0 copy-start.4
  125.5 2.6 %copy-start.1 = (f32[128,768]{1,0:T(8,128)S(1)}, f32[128,768]{1,0:T(8,128)}, u32[]{:S(2)}) copy-start(f32[128,768]{1,0:T(8,128)} %get-tuple-element.48) | copy-start | bytes 1179652
  126.4 0.9 copy-start.5
  128.0 1.1 copy-start

commit v2 on v1

--- a/solution.py
+++ b/solution.py
@@ -312,8 +312,9 @@
 
 def layer_kernel(
     ndp, heads,
-    tok, cot, gpad, gcol, wq, wo, wi, wd, cos_t, sin_t,
-    out_o, tg_o, gg_o, dq_o, do_o, di_o, dd_o,
+    tok, cot, gain_a, gain_b, wq_in, wo_in, wi_in, wd_in, cos_t, sin_t,
+    out_o, tg_o, ga_o, gb_o, dq_o, do_o, di_o, dd_o,
+    gpad, wq, wo, wi, wd,
     gains, wqf, wof, wif, wdf,
     x1, x2, xc, x3, xt1, xt2, xtc, xt3,
     qk, vb, att, pbuf, hid, actb, gateb, slopeb, lg, pg, gatt, dqs, dks, dvs,
@@ -378,6 +379,14 @@
         pl.semaphore_signal(barrier, inc=1, device_id=at_mp(other), device_id_type=MESH)
     pl.semaphore_wait(barrier, ndp - 1 + 3)
 
+    def place(gain):
+        row = jnp.concatenate(
+            [gain[...].astype(F32), jnp.zeros((1, width - shard), F32)], axis=1
+        )
+        return pltpu.roll(jnp.broadcast_to(row, (8, width)), dp * shard, 1)[0:1]
+
+    gpad[:, :width] = place(gain_a)
+    gpad[:, width:] = place(gain_b)
     gain_slots = [slot() for _ in range(ndp - 1)]
     for k in range(1, ndp):
         put(gpad, gains.at[dp], gain_slots[k - 1], at_dp(lax.rem(dp + k, ndp)))
@@ -454,6 +463,19 @@
             - normed * jnp.mean(scaled * normed, axis=-1, keepdims=True)
         )
 
+    def flip(vals):
+        high, wide = vals.shape
+        more_rows, more_cols = -high % 128, -wide % 128
+        if more_cols:
+            vals = jnp.concatenate([vals, jnp.zeros((high, more_cols), F32)], axis=1)
+        if more_rows:
+            vals = jnp.concatenate([vals, jnp.zeros((more_rows, wide + more_cols), F32)], axis=0)
+        return vals.T[:wide, :high]
+
+    def column(gain):
+        row = jnp.concatenate([gain[...].astype(F32), jnp.ones((1, 128 - shard), F32)], axis=1)
+        return jnp.broadcast_to(row, (128, 128)).T[:shard]
+
     def turn(buf, dst):
         @pl.loop(0, nmp)
         def _(r):
@@ -469,8 +491,11 @@
         for k in [*range(1, na), 0]:
             a = lax.rem(za + k, na)
             put(gs.at[a], gr.at[a], sems[k], at_dp(xpeer))
+        return (sems, gr, gw)
+
+    def grad_own(xt, right, gw):
+        cols = right.shape[1]
         gw[...] = nn(xt[:, zb].reshape(na * shard, length), right).reshape(na, shard, cols)
-        return (sems, gr, gw)
 
     def grad_middle(state, gz, gy):
         sems, gr, gw = state
@@ -494,6 +519,7 @@
     def tiles(count):
         return [slice(i * 128, (i + 1) * 128) for i in range(count)]
 
+    wq[...] = jnp.concatenate([wq_in[i] for i in range(3)], axis=1)
     ag_q = gather_start(wq, wqf)
     gains[dp] = gpad[...]
     for k in range(1, ndp):
@@ -510,7 +536,10 @@
     xh1[...] = normed_one
     x1[mp] = (normed_one * gain_one).astype(BF)
     sp1 = spread_start(x1)
+    wo[...] = flip(wo_in[...].astype(F32)).astype(BF)
     ag_o = gather_start(wo, wof)
+    wi[...] = jnp.concatenate([wi_in[:, i, :] for i in range(2)], axis=1)
+    wd[...] = flip(wd_in[...].astype(F32)).astype(BF)
     spread_forward(sp1)
     xc[mp] = cot[...]
     spc = spread_start(xc)
@@ -594,15 +623,20 @@
 
     rs_g = scatter_sum(1, in_part)
     g_d = grad_start(xtc, hid[...], gsd, grd, gwd)
+    grad_own(xtc, hid[...], gwd)
+    turn(x2, xt2)
     back_two = norm_back(scatter_end(rs_g), xh2[...], inv_two, gain_two)
     mgrad[...] = cot[...].astype(F32) + back_two
     x3[mp] = mgrad[...].astype(BF)
     sp3 = spread_start(x3)
-    turn(x2, xt2)
+    g_i = grad_start(xt2, lg[...], gsi, gri, gwi)
+    grad_own(xt2, lg[...], gwi)
+    rs_o = scatter_sum(3, down_part)
     spread_forward(sp3)
     g_d = grad_middle(g_d, gzd, gyd)
-    g_i = grad_start(xt2, lg[...], gsi, gri, gwi)
     spread_end(sp3)
+    turn(x3, xt3)
+    g_o = grad_start(xt3, att[...], gso, gro, gwo)
 
     dks[...] = jnp.zeros_like(dks)
     dvs[...] = jnp.zeros_like(dvs)
@@ -623,6 +657,8 @@
             dqs[h, at, :] = nn(ds, head(qk, heads + h))
             dks[h] += tn(ds, head(qk, h, at))
 
+    g_i = grad_middle(g_i, gzi, gyi)
+
     @pl.loop(0, nmp)
     def _(r):
         at = chunk(r)
@@ -642,33 +678,35 @@
         return nt(pg[chunk(r), :], wqf[...].reshape(width, 3 * local_width))
 
     rs_f = scatter_sum(2, qkv_part)
+    grad_own(xt1, pg[...], gwq)
+    grad_own(xt3, att[...], gwo)
+    g_o = grad_middle(g_o, gzo, gyo)
     g_q = grad_middle(g_q, gzq, gyq)
-    g_i = grad_middle(g_i, gzi, gyi)
-    rs_o = scatter_sum(3, down_part)
-    turn(x3, xt3)
-    g_o = grad_start(xt3, att[...], gso, gro, gwo)
     back_one = norm_back(scatter_end(rs_f), xh1[...], inv_one, gain_one)
     tg_o[...] = mgrad[...] + back_one
     out_o[...] = mixed[...] + scatter_end(rs_o)
-    g_o = grad_middle(g_o, gzo, gyo)
-    dd_o[...] = grad_end(g_d)
+    dd_o[...] = flip(grad_end(g_d))
     in_grad = grad_end(g_i)
-    di_o[...] = in_grad
+    for i in range(2):
+        di_o[:, i, :] = in_grad[:, i * units : (i + 1) * units]
+    sum_two = jnp.sum(in_grad * wi[...].astype(F32), axis=-1, keepdims=True)
+    do_o[...] = flip(grad_end(g_o))
     qkv_grad = grad_end(g_q)
-    dq_o[...] = qkv_grad
     sum_one = jnp.sum(qkv_grad * wq[...].astype(F32), axis=-1, keepdims=True)
-    sum_two = jnp.sum(in_grad * wi[...].astype(F32), axis=-1, keepdims=True)
-    lane = lax.broadcasted_iota(jnp.int32, gcol.shape, 1)
-    ggs[...] = jnp.where(lane < 64, sum_one, sum_two) / gcol[...]
+    lane = lax.broadcasted_iota(jnp.int32, (shard, 128), 1)
+    sums = jnp.where(lane < 1, sum_one / column(gain_a), sum_two / column(gain_b))
+    ggs[...] = flip(sums)[:8]
     gain_sems = [slot() for _ in range(3)]
     for k, other in enumerate((ypeer, mate, diag)):
         put(ggs, ggr.at[k], gain_sems[k], at_mp(other))
-    do_o[...] = grad_end(g_o)
+    for i in range(3):
+        dq_o[i] = qkv_grad[:, i * local_width : (i + 1) * local_width]
     total = ggs[...]
     for k in range(3):
         got(ggr.at[k], gain_sems[k])
         total = total + ggr[k]
-    gg_o[...] = total
+    ga_o[...] = total[0:1]
+    gb_o[...] = total[1:2]
     for copy in sends:
         copy.wait_send()
 
@@ -683,18 +721,6 @@
     heads = lw // HEAD_DIM
     length = rows * nmp
     na = ndp // PAIR
-    place = lax.axis_index("dp") * shard
-    pad = jnp.zeros((2, width), F32)
-    pad = lax.dynamic_update_slice(
-        pad, jnp.stack([attn_gain, mlp_gain]).astype(F32), (0, place)
-    ).reshape(1, 2 * width)
-    gcol = jnp.concatenate(
-        [
-            jnp.broadcast_to(attn_gain.astype(F32)[:, None], (shard, 64)),
-            jnp.broadcast_to(mlp_gain.astype(F32)[:, None], (shard, 64)),
-        ],
-        axis=1,
-    )
     half = HEAD_DIM // 2
     freqs = rope_base ** (-(np.arange(half, dtype=np.float32) * np.float32(2.0) / HEAD_DIM))
     angles = np.arange(length, dtype=np.float32)[:, None] * freqs.astype(np.float32)[None, :]
@@ -713,6 +739,8 @@
 
     nsem = 7 + 8 * na + 3 * 4 + 3 * 4 + 8 * na + 3 + 8
     scratch = [
+        buf((1, 2 * width), F32), buf((shard, 3 * lw)), buf((shard, lw)),
+        buf((shard, 2 * units)), buf((shard, units)),
         buf((ndp, 1, 2 * width), F32),
         buf((ndp, shard, 3 * lw)), buf((ndp, shard, lw)),
         buf((ndp, shard, 2 * units)), buf((ndp, shard, units)),
@@ -727,32 +755,30 @@
         buf((4, 2, rows, width)), buf((4, 2, rows, width)),
         buf((4, rows, width)), buf((4, rows, width)), buf((4, rows, width), F32),
         *grad_bufs(3 * lw), *grad_bufs(lw), *grad_bufs(2 * units), *grad_bufs(units),
-        buf((shard, 128), F32), buf((3, shard, 128), F32),
+        buf((8, shard), F32), buf((3, 8, shard), F32),
         pltpu.SemaphoreType.DMA((nsem,)), pltpu.SemaphoreType.DMA((nsem,)),
     ]
     vmem = pl.BlockSpec(memory_space=pltpu.VMEM)
     shapes = [
-        (rows, width), (rows, width), (shard, 128), (shard, 3 * lw), (shard, lw),
-        (shard, 2 * units), (shard, units),
+        (rows, width), (rows, width), (1, shard), (1, shard), (3, shard, lw), (lw, shard),
+        (shard, 2, units), (units, shard),
     ]
-    out, tg, gg, dq, do, di, dd = pl.pallas_call(
+    out, tg, ga, gb, dq, do, di, dd = pl.pallas_call(
         functools.partial(layer_kernel, ndp, heads),
         out_shape=[jax.ShapeDtypeStruct(s, F32) for s in shapes],
         in_specs=[vmem] * 10,
-        out_specs=[vmem] * 7,
+        out_specs=[vmem] * 8,
         scratch_shapes=scratch,
         compiler_params=pltpu.CompilerParams(
             collective_id=0, has_side_effects=True, vmem_limit_bytes=60 * 1024 * 1024
         ),
     )(
-        tokens, cotangent, pad.reshape(1, 2 * width), gcol,
-        w_qkv.reshape(shard, 3 * lw), w_attn_out.T,
-        w_in.reshape(shard, 2 * units), w_mlp_out.T,
+        tokens, cotangent, attn_gain.reshape(1, shard), mlp_gain.reshape(1, shard),
+        w_qkv.transpose(1, 0, 2), w_attn_out, w_in, w_mlp_out,
         jnp.asarray(cos_t), jnp.asarray(sin_t),
     )
     return (
-        out, tg, gg[:, 0], dq.reshape(shard, 3, lw), do.T, gg[:, 64],
-        di.reshape(shard, 2, units), dd.T,
+        out, tg, ga.reshape(shard), dq.transpose(1, 0, 2), do, gb.reshape(shard), di, dd,
     )
 
 
@@ -763,6 +789,7 @@
         lax.axis_size("mp") == 4
         and ndp % PAIR == 0
         and shard % 16 == 0
+        and shard <= 128
         and w_mlp_out.shape[1] == shard
         and tokens.shape[0] % 128 == 0
         and tokens.shape[0] <= 128

time: 132 us -> 117 us (0.89)
  local copies, waits for them, and re-layouts: 14.1 us -> 6.88 us
  Pallas kernels: 114 us -> 108 us
    pallas_call x1, Pallas kernels: 114 us -> 108 us  [fused_shards(): pl.pallas_call(functools.partial(layer_kernel, ndp, heads), out_shape=[ja...]
    reshape x3 -> x0, local copies, waits for them, and re-layouts: 2.53 us -> none  [the longest x1 0.95 us: fused_shards(): di.reshape(shard, 2, units)]
    slice x1 -> x0, local copies, waits for them, and re-layouts: 1.58 us -> none  [fused_shards(): gg[:, 64]]
    unnamed x29 -> x22, local copies, waits for them, and re-layouts: 8.44 us -> 6.88 us
where the time goes in v2:
time: 117 us; the launch traced here: 116 us
  Pallas kernels  108 us (92%)
  local copies, waits for them, and re-layouts  6.88 us (6%)
    pallas_call x1, Pallas kernels, fused_shards(): pl.pallas_call(functools.partial(layer_kernel, ndp, heads), out_shape=[ja...  108 us
    unnamed x22, local copies, waits for them, and re-layouts  6.88 us

profile of v2, /device:TPU:25, one launch (start us, length us, event | category | flops | bytes accessed | tf_op | source)
XLA Modules:
  0.0 116.0 jit_solution(4955047537405787553)
XLA Ops:
  0.6 108.5 %shard_map.161 = (f32[128,768]{1,0:T(8,128)}, f32[128,768]{1,0:T(8,128)}, f32[1,96]{1,0:T(1,128)}, f32[1,96]{1,0:T(1,128)}, f32[3,96,192]{2,1,0:T(8,128)}, /*ind...) custom-call(bf16[128,768]{1,0:T(8,128)(2,1)} %tok.1, bf16[128,768]{1,0:T(8,128)(2,1)} %cot.1, ...), custom_call_target="tpu_custom_call" | custom-call | tf_op jit(solution)/shard_map/pallas_call | solution.py:766
  109.1 0.0 copy-start
  109.2 1.8 %copy.26 = f32[128,768]{1,0:T(8,128)} copy(f32[128,768]{1,0:T(8,128)} %get-tuple-element.32) | data formatting | bytes 786432
  111.0 0.0 copy-done
  111.0 0.0 copy-start.6
  111.0 0.0 copy-start.2
  111.0 0.7 copy.27
  111.7 0.0 copy-done.6
  111.7 0.5 copy.28
  112.2 0.0 copy-done.2
  112.2 0.0 copy-start.4
  112.2 0.0 copy-start.1
  112.2 0.7 copy.29
  113.0 0.2 copy-done.4
  113.2 0.0 copy-start.5
  113.2 0.6 copy.30
  113.8 0.0 copy-done.5
  113.8 0.5 copy.31
  114.4 0.0 copy-done.1
  114.4 0.0 copy-start.3
  114.4 0.7 copy.32
  115.1 0.3 copy-done.3
  115.4 0.7 copy.33
Async XLA Ops:
  109.1 1.8 %copy-start = (f32[128,768]{1,0:T(8,128)S(1)}, f32[128,768]{1,0:T(8,128)}, u32[]{:S(2)}) copy-start(f32[128,768]{1,0:T(8,128)} %get-tuple-element.33) | copy-start | bytes 1179652
  111.0 0.8 copy-start.6
  111.0 1.3 %copy-start.2 = (f32[3,96,192]{2,1,0:T(8,128)S(1)}, f32[3,96,192]{2,1,0:T(8,128)}, u32[]{:S(2)}) copy-start(f32[3,96,192]{2,1,0:T(8,128)} %get-tuple-element.19) | copy-start | bytes 663556
  112.2 1.0 copy-start.4
  112.2 2.1 %copy-start.1 = (f32[96,2,288]{2,1,0:T(2,128)S(1)}, f32[96,2,288]{2,1,0:T(2,128)}, u32[]{:S(2)}) copy-start(f32[96,2,288]{2,1,0:T(2,128)} %get-tuple-element.38) | copy-start | bytes 663556
  113.2 0.6 copy-start.5
  114.4 1.0 copy-start.3

commit v3 on v2

--- a/solution.py
+++ b/solution.py
@@ -10,6 +10,7 @@
 
 MESH = pl.DeviceIdType.MESH
 PAIR = 2
+PARTS = 2
 BF = jnp.bfloat16
 F32 = jnp.float32
 
@@ -317,7 +318,7 @@
     gpad, wq, wo, wi, wd,
     gains, wqf, wof, wif, wdf,
     x1, x2, xc, x3, xt1, xt2, xtc, xt3,
-    qk, vb, att, pbuf, hid, actb, gateb, slopeb, lg, pg, gatt, dqs, dks, dvs,
+    qk, vb, att, pbuf, hid, wide, hgrad_buf, lg, pg, gatt, dqs, dks, dvs,
     xh1, xh2, mixed, mgrad,
     rs_sc, rs_rc, rs_sy, rs_ry, rs_own,
     gsq, grq, gzq, gyq, gwq,
@@ -413,42 +414,67 @@
             source = lax.rem(za + na - k, na) * PAIR + (1 - zb)
             got(full.at[source], xs[k])
 
-    def spread_start(buf):
-        sems = [slot() for _ in range(3)]
-        put(buf.at[mp], buf.at[mp], sems[0], at_mp(ypeer))
-        put(buf.at[mp], buf.at[mp], sems[1], at_mp(mate))
-        return (buf, sems)
+    part_rows = rows // PARTS
+
+    def part_at(p):
+        return pl.ds(p * part_rows, part_rows)
+
+    def spread_open(buf):
+        return (buf, [[slot() for _ in range(3)] for _ in range(PARTS)])
+
+    def spread_start(state, p):
+        buf, sems = state
+        block = buf.at[mp, part_at(p)]
+        put(block, block, sems[p][0], at_mp(ypeer))
+        put(block, block, sems[p][1], at_mp(mate))
 
     def spread_forward(state):
         buf, sems = state
-        got(buf.at[ypeer], sems[0])
-        put(buf.at[ypeer], buf.at[ypeer], sems[2], at_mp(mate))
-        got(buf.at[mate], sems[1])
+        for p in range(PARTS):
+            block = buf.at[ypeer, part_at(p)]
+            got(block, sems[p][0])
+            put(block, block, sems[p][2], at_mp(mate))
 
     def spread_end(state):
         buf, sems = state
-        got(buf.at[diag], sems[2])
-
-    def scatter_sum(i, part):
-        s0, s1, s2 = slot(), slot(), slot()
-        far_mate = 2 * (1 - ypos) + (1 - core)
-        rs_sc[i, 0] = part(far_mate).astype(BF)
-        put(rs_sc.at[i, 0], rs_rc.at[i, 0], s0, at_mp(mate))
-        rs_sc[i, 1] = part(mate).astype(BF)
-        put(rs_sc.at[i, 1], rs_rc.at[i, 1], s1, at_mp(mate))
-        far = part(ypeer)
-        got(rs_rc.at[i, 0], s0)
-        rs_sy[i] = (far + rs_rc[i, 0].astype(F32)).astype(BF)
-        put(rs_sy.at[i], rs_ry.at[i], s2, at_mp(ypeer))
-        rs_own[i] = part(mp)
-        return (i, s1, s2)
-
-    def scatter_end(state):
-        i, s1, s2 = state
-        got(rs_rc.at[i, 1], s1)
-        near = rs_own[i] + rs_rc[i, 1].astype(F32)
-        got(rs_ry.at[i], s2)
-        return near + rs_ry[i].astype(F32)
+        for p in range(PARTS):
+            got(buf.at[mate, part_at(p)], sems[p][1])
+            got(buf.at[diag, part_at(p)], sems[p][2])
+
+    def core_rows(ref, c):
+        return jnp.concatenate([ref[chunk(c), :], ref[chunk(2 + c), :]], axis=0)
+
+    def scatter_sum(i, left, weights):
+        s_far = [slot() for _ in range(PARTS)]
+        s_near = slot()
+        s_y = [slot() for _ in range(PARTS)]
+        other = nt(core_rows(left, 1 - core), weights)
+        rs_sc[i] = other.astype(BF).reshape(2, rows, width)
+        for p in range(PARTS):
+            at = part_at(p)
+            put(rs_sc.at[i, 1 - ypos, at], rs_rc.at[i, 1 - ypos, at], s_far[p], at_mp(mate))
+        put(rs_sc.at[i, ypos], rs_rc.at[i, ypos], s_near, at_mp(mate))
+        rs_own[i] = nt(core_rows(left, core), weights).reshape(2, rows, width)
+        for p in range(PARTS):
+            at = part_at(p)
+            got(rs_rc.at[i, 1 - ypos, at], s_far[p])
+            rs_sy[i, at, :] = (
+                rs_own[i, 1 - ypos, at, :] + rs_rc[i, 1 - ypos, at, :].astype(F32)
+            ).astype(BF)
+            put(rs_sy.at[i, at], rs_ry.at[i, at], s_y[p], at_mp(ypeer))
+        return (i, s_near, s_y)
+
+    def scatter_end(state, p):
+        i, s_near, s_y = state
+        at = part_at(p)
+        if p == 0:
+            got(rs_rc.at[i, ypos], s_near)
+        near = rs_own[i, ypos, at, :] + rs_rc[i, ypos, at, :].astype(F32)
+        got(rs_ry.at[i, at], s_y[p])
+        return near + rs_ry[i, at, :].astype(F32)
+
+    def chunk(r):
+        return pl.ds(pl.multiple_of(r * rows, rows), rows)
 
     def norm(vals):
         centered = vals - jnp.mean(vals, axis=-1, keepdims=True)
@@ -535,14 +561,18 @@
     normed_one, inv_one = norm(residual)
     xh1[...] = normed_one
     x1[mp] = (normed_one * gain_one).astype(BF)
-    sp1 = spread_start(x1)
+    sp1 = spread_open(x1)
+    for p in range(PARTS):
+        spread_start(sp1, p)
     wo[...] = flip(wo_in[...].astype(F32)).astype(BF)
     ag_o = gather_start(wo, wof)
     wi[...] = jnp.concatenate([wi_in[:, i, :] for i in range(2)], axis=1)
     wd[...] = flip(wd_in[...].astype(F32)).astype(BF)
     spread_forward(sp1)
     xc[mp] = cot[...]
-    spc = spread_start(xc)
+    spc = spread_open(xc)
+    for p in range(PARTS):
+        spread_start(spc, p)
     gather_forward(ag_q)
     ag_i = gather_start(wi, wif)
     ag_d = gather_start(wd, wdf)
@@ -553,14 +583,17 @@
     turn(xc, xtc)
     gather_end(ag_q)
 
+    wide[:, : 3 * local_width] = nn(
+        x1[...].reshape(length, width), wqf[...].reshape(width, 3 * local_width)
+    )
+
     @pl.loop(0, nmp)
     def _(r):
-        at = pl.ds(pl.multiple_of(r * rows, rows), rows)
-        proj = nn(x1[r], wqf[...].reshape(width, 3 * local_width))
+        at = chunk(r)
         for t in tiles(2 * local_width // 128):
-            u = proj[:, t]
+            u = wide[at, t]
             qk[at, t] = (u * cos_t[at, :] + swap_halves(u) * sin_t[at, :]).astype(BF)
-        vb[at, :] = proj[:, 2 * local_width :].astype(BF)
+        vb[at, :] = wide[at, 2 * local_width : 3 * local_width].astype(BF)
 
     gather_forward(ag_o)
     scale = HEAD_DIM ** (-0.5)
@@ -568,9 +601,11 @@
     def head(ref, h, at=slice(None)):
         return ref[at, h * HEAD_DIM : (h + 1) * HEAD_DIM]
 
-    @pl.loop(0, nmp)
+    block = 2 * rows
+
+    @pl.loop(0, length // block)
     def _(r):
-        at = pl.ds(pl.multiple_of(r * rows, rows), rows)
+        at = pl.ds(pl.multiple_of(r * block, block), block)
         outs = []
         for h in range(heads):
             scores = nt(head(qk, h, at), head(qk, heads + h)) * scale
@@ -583,55 +618,54 @@
 
     gather_end(ag_o)
 
-    def chunk(r):
-        return pl.ds(pl.multiple_of(r * rows, rows), rows)
-
-    def attn_part(r):
-        return nt(att[chunk(r), :], wof[...].reshape(width, local_width))
-
-    rs_a = scatter_sum(0, attn_part)
+    rs_a = scatter_sum(0, att, wof[...].reshape(width, local_width))
     gather_forward(ag_i)
+    inv_two = []
+    sp2 = spread_open(x2)
+    for p in range(PARTS):
+        at = part_at(p)
+        mixed[at, :] = tok[at, :].astype(F32) + scatter_end(rs_a, p)
+        normed_two, inv = norm(mixed[at, :])
+        inv_two.append(inv)
+        xh2[at, :] = normed_two
+        x2[mp, at, :] = (normed_two * gain_two).astype(BF)
+        spread_start(sp2, p)
+    spread_forward(sp2)
     gather_forward(ag_d)
-    mixed[...] = residual + scatter_end(rs_a)
-    normed_two, inv_two = norm(mixed[...])
-    xh2[...] = normed_two
-    x2[mp] = (normed_two * gain_two).astype(BF)
-    sp2 = spread_start(x2)
     gather_end(ag_i)
     gather_end(ag_d)
-    spread_forward(sp2)
+    hgrad_buf[...] = nn(xc[...].reshape(length, width), wdf[...].reshape(width, units))
     spread_end(sp2)
+    wide[:, : 2 * units] = nn(
+        x2[...].reshape(length, width), wif[...].reshape(width, 2 * units)
+    )
 
     @pl.loop(0, nmp)
     def _(r):
         at = chunk(r)
-        lifted = nn(x2[r], wif[...].reshape(width, 2 * units))
-        u = lifted[:, :units]
-        gate = lifted[:, units:]
+        u = wide[at, :units]
+        gate = wide[at, units : 2 * units]
         cdf = 0.5 * (1.0 + erf(u * 0.7071067811865476))
         act = u * cdf
         slope = cdf + u * jnp.exp(-0.5 * u * u) * 0.3989422804014327
         hid[at, :] = (act * gate).astype(BF)
-        hgrad = nn(xc[r], wdf[...].reshape(width, units))
+        hgrad = hgrad_buf[at, :]
         lg[at, :] = jnp.concatenate([hgrad * gate * slope, hgrad * act], axis=1).astype(BF)
 
-    def in_part(r):
-        return nt(lg[chunk(r), :], wif[...].reshape(width, 2 * units))
-
-    def down_part(r):
-        return nt(hid[chunk(r), :], wdf[...].reshape(width, units))
-
-    rs_g = scatter_sum(1, in_part)
+    rs_g = scatter_sum(1, lg, wif[...].reshape(width, 2 * units))
     g_d = grad_start(xtc, hid[...], gsd, grd, gwd)
     grad_own(xtc, hid[...], gwd)
     turn(x2, xt2)
-    back_two = norm_back(scatter_end(rs_g), xh2[...], inv_two, gain_two)
-    mgrad[...] = cot[...].astype(F32) + back_two
-    x3[mp] = mgrad[...].astype(BF)
-    sp3 = spread_start(x3)
+    sp3 = spread_open(x3)
+    for p in range(PARTS):
+        at = part_at(p)
+        back_two = norm_back(scatter_end(rs_g, p), xh2[at, :], inv_two[p], gain_two)
+        mgrad[at, :] = cot[at, :].astype(F32) + back_two
+        x3[mp, at, :] = mgrad[at, :].astype(BF)
+        spread_start(sp3, p)
     g_i = grad_start(xt2, lg[...], gsi, gri, gwi)
     grad_own(xt2, lg[...], gwi)
-    rs_o = scatter_sum(3, down_part)
+    rs_o = scatter_sum(3, hid, wdf[...].reshape(width, units))
     spread_forward(sp3)
     g_d = grad_middle(g_d, gzd, gyd)
     spread_end(sp3)
@@ -641,10 +675,14 @@
     dks[...] = jnp.zeros_like(dks)
     dvs[...] = jnp.zeros_like(dvs)
 
-    @pl.loop(0, nmp)
+    gatt[...] = nn(
+        x3[...].reshape(length, width), wof[...].reshape(width, local_width)
+    ).astype(BF)
+
+    @pl.loop(0, length // block)
     def _(r):
-        at = chunk(r)
-        agrad = nn(x3[r], wof[...].reshape(width, local_width)).astype(BF)
+        at = pl.ds(pl.multiple_of(r * block, block), block)
+        agrad = gatt[at, :]
         out_rows = att[at, :]
         for h in range(heads):
             g = agrad[:, h * HEAD_DIM : (h + 1) * HEAD_DIM]
@@ -674,17 +712,17 @@
 
     g_q = grad_start(xt1, pg[...], gsq, grq, gwq)
 
-    def qkv_part(r):
-        return nt(pg[chunk(r), :], wqf[...].reshape(width, 3 * local_width))
-
-    rs_f = scatter_sum(2, qkv_part)
+    rs_f = scatter_sum(2, pg, wqf[...].reshape(width, 3 * local_width))
     grad_own(xt1, pg[...], gwq)
     grad_own(xt3, att[...], gwo)
     g_o = grad_middle(g_o, gzo, gyo)
     g_q = grad_middle(g_q, gzq, gyq)
-    back_one = norm_back(scatter_end(rs_f), xh1[...], inv_one, gain_one)
-    tg_o[...] = mgrad[...] + back_one
-    out_o[...] = mixed[...] + scatter_end(rs_o)
+    for p in range(PARTS):
+        at = part_at(p)
+        own_inv = inv_one[p * part_rows : (p + 1) * part_rows]
+        back_one = norm_back(scatter_end(rs_f, p), xh1[at, :], own_inv, gain_one)
+        tg_o[at, :] = mgrad[at, :] + back_one
+        out_o[at, :] = mixed[at, :] + scatter_end(rs_o, p)
     dd_o[...] = flip(grad_end(g_d))
     in_grad = grad_end(g_i)
     for i in range(2):
@@ -711,6 +749,12 @@
         copy.wait_send()
 
 
+def settle_kernel(*refs):
+    count = len(refs) // 2
+    for src, dst in zip(refs[:count], refs[count:]):
+        dst[...] = src[...]
+
+
 def fused_shards(tokens, cotangent, attn_gain, w_qkv, w_attn_out, mlp_gain, w_in, w_mlp_out):
     ndp = lax.axis_size("dp")
     nmp = lax.axis_size("mp")
@@ -737,7 +781,7 @@
             buf((na, shard, cols)), buf((na, shard, cols), F32),
         ]
 
-    nsem = 7 + 8 * na + 3 * 4 + 3 * 4 + 8 * na + 3 + 8
+    nsem = ndp + 16 * na + 4 * (3 * PARTS) + 4 * (2 * PARTS + 1) + 8
     scratch = [
         buf((1, 2 * width), F32), buf((shard, 3 * lw)), buf((shard, lw)),
         buf((shard, 2 * units)), buf((shard, units)),
@@ -748,12 +792,12 @@
         *[buf((na, PAIR, shard, length)) for _ in range(4)],
         buf((length, 2 * lw)), buf((length, lw)), buf((length, lw)),
         buf((heads, length, length), F32), buf((length, units)),
-        buf((8, 128)), buf((8, 128)), buf((8, 128)),
-        buf((length, 2 * units)), buf((length, 3 * lw)), buf((8, 128)),
+        buf((length, max(3 * lw, 2 * units)), F32), buf((length, units), F32),
+        buf((length, 2 * units)), buf((length, 3 * lw)), buf((length, lw)),
         *[buf((heads, length, HEAD_DIM), F32) for _ in range(3)],
         *[buf((rows, width), F32) for _ in range(4)],
         buf((4, 2, rows, width)), buf((4, 2, rows, width)),
-        buf((4, rows, width)), buf((4, rows, width)), buf((4, rows, width), F32),
+        buf((4, rows, width)), buf((4, rows, width)), buf((4, 2, rows, width), F32),
         *grad_bufs(3 * lw), *grad_bufs(lw), *grad_bufs(2 * units), *grad_bufs(units),
         buf((8, shard), F32), buf((3, 8, shard), F32),
         pltpu.SemaphoreType.DMA((nsem,)), pltpu.SemaphoreType.DMA((nsem,)),
@@ -777,6 +821,12 @@
         w_qkv.transpose(1, 0, 2), w_attn_out, w_in, w_mlp_out,
         jnp.asarray(cos_t), jnp.asarray(sin_t),
     )
+    out, tg, ga, gb, dq, do, di, dd = pl.pallas_call(
+        settle_kernel,
+        out_shape=[jax.ShapeDtypeStruct(s, F32) for s in shapes],
+        in_specs=[vmem] * 8,
+        out_specs=[vmem] * 8,
+    )(out, tg, ga, gb, dq, do, di, dd)
     return (
         out, tg, ga.reshape(shard), dq.transpose(1, 0, 2), do, gb.reshape(shard), di, dd,
     )

time: 117 us -> 110 us (0.940)
  local copies, waits for them, and re-layouts: 6.88 us -> 0 us
    unnamed x22 -> x0, local copies, waits for them, and re-layouts: 6.88 us -> none
    pallas_call x0 -> x1, Pallas kernels: none -> 2.57 us  [fused_shards(): pl.pallas_call(settle_kernel, out_shape=[jax.ShapeDtypeStruct(s, F32) for...]
    pallas_call x1, Pallas kernels: 108 us -> 107 us  [fused_shards(): pl.pallas_call(functools.partial(layer_kernel, ndp, heads), out_shape=[ja...]
where the time goes in v3:
time: 110 us
  Pallas kernels  109 us (99%)
    pallas_call x1, Pallas kernels, fused_shards(): pl.pallas_call(functools.partial(layer_kernel, ndp, heads), out_shape=[ja...  107 us
    pallas_call x1, Pallas kernels, fused_shards(): pl.pallas_call(settle_kernel, out_shape=[jax.ShapeDtypeStruct(s, F32) for...  2.57 us

profile of v3, /device:TPU:25, one launch (start us, length us, event | category | flops | bytes accessed | tf_op | source)
XLA Modules:
  0.0 109.8 jit_solution(16318725331741110281)
XLA Ops:
  0.6 106.5 %shard_map.161 = (f32[128,768]{1,0:T(8,128)}, f32[128,768]{1,0:T(8,128)}, f32[1,96]{1,0:T(1,128)}, f32[1,96]{1,0:T(1,128)}, f32[3,96,192]{2,1,0:T(8,128)}, /*ind...) custom-call(bf16[128,768]{1,0:T(8,128)(2,1)} %tok.1, bf16[128,768]{1,0:T(8,128)(2,1)} %cot.1, ...), custom_call_target="tpu_custom_call" | custom-call | tf_op jit(solution)/shard_map/pallas_call | solution.py:810
  107.2 2.6 %shard_map.162 = (f32[128,768]{1,0:T(8,128)}, f32[128,768]{1,0:T(8,128)}, f32[1,96]{1,0:T(1,128)}, f32[1,96]{1,0:T(1,128)}, f32[3,96,192]{2,1,0:T(8,128)}, /*ind...) custom-call(f32[128,768]{1,0:T(8,128)} %get-tuple-element.24.refs_0_, ...), custom_call_target="tpu_custom_call" | custom-call | tf_op jit(solution)/shard_map/pallas_call | solution.py:824

commit v4 on v3

--- a/solution.py
+++ b/solution.py
@@ -630,15 +630,16 @@
         xh2[at, :] = normed_two
         x2[mp, at, :] = (normed_two * gain_two).astype(BF)
         spread_start(sp2, p)
+    gather_forward(ag_d)
     spread_forward(sp2)
-    gather_forward(ag_d)
     gather_end(ag_i)
-    gather_end(ag_d)
-    hgrad_buf[...] = nn(xc[...].reshape(length, width), wdf[...].reshape(width, units))
     spread_end(sp2)
     wide[:, : 2 * units] = nn(
         x2[...].reshape(length, width), wif[...].reshape(width, 2 * units)
     )
+    turn(x2, xt2)
+    gather_end(ag_d)
+    hgrad_buf[...] = nn(xc[...].reshape(length, width), wdf[...].reshape(width, units))
 
     @pl.loop(0, nmp)
     def _(r):
@@ -654,8 +655,8 @@
 
     rs_g = scatter_sum(1, lg, wif[...].reshape(width, 2 * units))
     g_d = grad_start(xtc, hid[...], gsd, grd, gwd)
+    g_i = grad_start(xt2, lg[...], gsi, gri, gwi)
     grad_own(xtc, hid[...], gwd)
-    turn(x2, xt2)
     sp3 = spread_open(x3)
     for p in range(PARTS):
         at = part_at(p)
@@ -663,7 +664,6 @@
         mgrad[at, :] = cot[at, :].astype(F32) + back_two
         x3[mp, at, :] = mgrad[at, :].astype(BF)
         spread_start(sp3, p)
-    g_i = grad_start(xt2, lg[...], gsi, gri, gwi)
     grad_own(xt2, lg[...], gwi)
     rs_o = scatter_sum(3, hid, wdf[...].reshape(width, units))
     spread_forward(sp3)
@@ -679,9 +679,8 @@
         x3[...].reshape(length, width), wof[...].reshape(width, local_width)
     ).astype(BF)
 
-    @pl.loop(0, length // block)
-    def _(r):
-        at = pl.ds(pl.multiple_of(r * block, block), block)
+    for r in range(length // block):
+        at = pl.ds(r * block, block)
         agrad = gatt[at, :]
         out_rows = att[at, :]
         for h in range(heads):
@@ -694,8 +693,11 @@
             ds = (probs * (dprobs - delta) * scale).astype(BF)
             dqs[h, at, :] = nn(ds, head(qk, heads + h))
             dks[h] += tn(ds, head(qk, h, at))
-
-    g_i = grad_middle(g_i, gzi, gyi)
+        if r == 0:
+            g_i = grad_middle(g_i, gzi, gyi)
+
+    grad_own(xt3, att[...], gwo)
+    g_o = grad_middle(g_o, gzo, gyo)
 
     @pl.loop(0, nmp)
     def _(r):
@@ -714,8 +716,6 @@
 
     rs_f = scatter_sum(2, pg, wqf[...].reshape(width, 3 * local_width))
     grad_own(xt1, pg[...], gwq)
-    grad_own(xt3, att[...], gwo)
-    g_o = grad_middle(g_o, gzo, gyo)
     g_q = grad_middle(g_q, gzq, gyq)
     for p in range(PARTS):
         at = part_at(p)

time: 110 us -> 106 us (0.964); the launches traced: 110 us -> 104 us
  Pallas kernels: 109 us -> 103 us
    pallas_call x1, Pallas kernels: 107 us -> 101 us  [fused_shards(): pl.pallas_call(functools.partial(layer_kernel, ndp, heads), out_shape=[ja...]
where the time goes in v4:
time: 106 us; the launch traced here: 104 us
  Pallas kernels  103 us (97%)
    pallas_call x1, Pallas kernels, fused_shards(): pl.pallas_call(functools.partial(layer_kernel, ndp, heads), out_shape=[ja...  101 us
    pallas_call x1, Pallas kernels, fused_shards(): pl.pallas_call(settle_kernel, out_shape=[jax.ShapeDtypeStruct(s, F32) for...  2.57 us

profile of v4, /device:TPU:25, one launch (start us, length us, event | category | flops | bytes accessed | tf_op | source)
XLA Modules:
  0.0 104.0 jit_solution(2490353071380604188)
XLA Ops:
  0.6 100.8 %shard_map.161 = (f32[128,768]{1,0:T(8,128)}, f32[128,768]{1,0:T(8,128)}, f32[1,96]{1,0:T(1,128)}, f32[1,96]{1,0:T(1,128)}, f32[3,96,192]{2,1,0:T(8,128)}, /*ind...) custom-call(bf16[128,768]{1,0:T(8,128)(2,1)} %tok.1, bf16[128,768]{1,0:T(8,128)(2,1)} %cot.1, ...), custom_call_target="tpu_custom_call" | custom-call | tf_op jit(solution)/shard_map/pallas_call | solution.py:810
  101.5 2.6 %shard_map.162 = (f32[128,768]{1,0:T(8,128)}, f32[128,768]{1,0:T(8,128)}, f32[1,96]{1,0:T(1,128)}, f32[1,96]{1,0:T(1,128)}, f32[3,96,192]{2,1,0:T(8,128)}, /*ind...) custom-call(f32[128,768]{1,0:T(8,128)} %get-tuple-element.24.refs_0_, ...), custom_call_target="tpu_custom_call" | custom-call | tf_op jit(solution)/shard_map/pallas_call | solution.py:824
